TPU v7x, 128 devices: a whole 4x4x4 slice. The times are simulated.
128 devices in a mesh: fx: 16 (over x, z), fy: 8 (over y, core).
Axes of the slice: x: 4, y: 4, z: 4, core: 2. Of those that a mesh axis runs over, the one named last changes fastest.
Arguments:
- fluid_state: float32 [5, 8, 2048, 1024], P(None, None, 'fx', 'fy'), may hold values from -0.3 to 2.8, as said below
- surface_points: float32 [16384, 3, 128], P(('fx', 'fy')), may hold values from 0 to 1
- surface_normals: float32 [16384, 3, 128], P(('fx', 'fy')), may hold values from -1 to 1
- owner_ids: int32 [16384, 1], P(('fx', 'fy')), may hold values from 0 to 127; in each aligned block of 128 rows (0 to 127, 128 to 255, ...) at most 2 rows name the same one
- support_ids: int32 [16384, 2], P(('fx', 'fy')), may hold values from 0 to 7
- struct_points: float32 [1024, 3, 128], P(('fx', 'fy')), may hold values from 0 to 1
- couplings: float32 [1024, 4, 128, 128], P(('fx', 'fy')), may hold values from 0.5 to 1
- coupling_pattern: int32 [1024, 4], P(('fx', 'fy')), may hold values from 0 to 7, as said below
- stiff_diagonal: float32 [1024, 128], P(('fx', 'fy')), may hold values from 1.05 to 1.6
- struct_load: float32 [1024, 3, 128], P(('fx', 'fy')), may hold values from -6 to 6
- predicted: float32 [1024, 3, 128], P(('fx', 'fy')), may hold values from -3 to 3
- hist_residual: float32 [8, 1024, 3, 128], P(None, ('fx', 'fy')), may hold values from -0.03 to 0.03
- hist_response: float32 [8, 1024, 3, 128], P(None, ('fx', 'fy')), may hold values from -6 to 6
Outputs:
- new_state: float32 [5, 8, 2048, 1024], P(None, None, 'fx', 'fy')
- next_estimate: float32 [1024, 3, 128], P(('fx', 'fy'))
- coupling_residual: float32 [1024, 3, 128], P(('fx', 'fy'))
Inputs may be any that keep to these rules, and one draw needn't show every extreme that they name: `fluid_state`: component 0 (density) lies in [0.8, 1.2], components 1 to 3 (momenta) in [-0.3, 0.3], component 4 (total energy) in [2.2, 2.8]. `owner_ids`: among the 128 surface blocks of one device (aligned blocks of rows), no owner is named by more than 2 of them. `support_ids`: local block numbers on the owner. For each device's 8 structure blocks and each column k, the entries coupling_pattern[., k] are a permutation of 0 to 7.
All inputs are finite; a program needn't handle non-finite values.
Results may differ from a plain program's by a relative error of at most 0.0003.
Values sent between devices are 32-bit elements; how exact they have to be, the bound alone decides.
No kernel may reach another device: no remote copies, remote signals or barrier semaphores. Data moves between devices by JAX's collectives and lax.ppermute only.
A program may use at most 192 MiB of HBM per device.

v0:
```python
import functools

import jax
import jax.numpy as jnp
from jax import lax
from jax.experimental import pallas as pl
from jax.experimental.pallas import tpu as pltpu
from jax.sharding import PartitionSpec as P

AXES = ("fx", "fy")
DEVICES = 128
TOP_PRECISION = lax.Precision.HIGHEST
STEP_RATIO = 0.12
WALL_SPEED = 0.5
WALL_GAIN = 0.5
LOAD_SCALE = 4.0
PRESSURE_REF = 0.98
SHIFT = 1.25
PEERS = 4
F32 = jnp.float32
BF16 = jnp.bfloat16
VMEM = pltpu.VMEM
SMEM = pltpu.SMEM


def iota(shape, dim):
    return lax.broadcasted_iota(jnp.int32, shape, dim)


def edges_kernel(state, low_x, high_x, low_y, high_y):
    lanes = iota((128, 128), 1)
    first = jnp.zeros((128, 128), F32)
    final = jnp.zeros((128, 128), F32)
    for part in range(5):
        for z in range(8):
            line = part * 8 + z
            low_x[line : line + 1, :] = state[part, z, 0:1, :]
            high_x[line : line + 1, :] = state[part, z, 127:128, :]
            first = jnp.where(lanes == line, state[part, z, :, 0:1], first)
            final = jnp.where(lanes == line, state[part, z, :, 127:128], final)
    low_y[...] = first.T[:40]
    high_y[...] = final.T[:40]


def cell_terms(state):
    inverse = 1.0 / state[0]
    pressure = 0.4 * (
        state[4]
        - 0.5 * (state[1] * state[1] + state[2] * state[2] + state[3] * state[3]) * inverse
    )
    return inverse, pressure, jnp.sqrt(1.4 * pressure * inverse)


def flux_terms(state, terms, momentum):
    inverse, pressure, sound = terms
    velocity = state[momentum] * inverse
    flux = [part * velocity for part in state]
    flux[momentum] = flux[momentum] + pressure
    flux[4] = flux[4] + pressure * velocity
    return flux, jnp.abs(velocity) + sound


def face(left, right):
    (left_state, (left_flux, left_speed)), (right_state, (right_flux, right_speed)) = left, right
    half = 0.5 * jnp.maximum(left_speed, right_speed)
    return [
        0.5 * (left_flux[part] + right_flux[part])
        - half * (right_state[part] - left_state[part])
        for part in range(5)
    ]


def fluid_kernel(levels, state, low_x, high_x, low_y, high_y, *refs):
    base, sides = refs[-2:]
    lanes = iota((128, 128), 1)
    filler = jnp.zeros((88, 128), F32)
    low_cols = jnp.concatenate([low_y[...], filler], axis=0).T
    high_cols = jnp.concatenate([high_y[...], filler], axis=0).T
    for level, z in enumerate(levels):
        for part in range(5):
            line = part * 8 + z
            tile = state[part, z]
            sides[0, part] = jnp.concatenate([low_x[line : line + 1, :], tile[:127]], axis=0)
            sides[1, part] = jnp.concatenate([tile[1:], high_x[line : line + 1, :]], axis=0)
            sides[2, part] = jnp.where(
                lanes == 0, low_cols[:, line : line + 1], pltpu.roll(tile, 1, 1)
            )
            sides[3, part] = jnp.where(
                lanes == 127, high_cols[:, line : line + 1], pltpu.roll(tile, 127, 1)
            )

        def body(chunk, carry):
            rows = pl.ds(pl.multiple_of(chunk * 8, 8), 8)
            middle = [state[part, z, rows, :] for part in range(5)]
            own = cell_terms(middle)
            change = None
            for axis in range(2):
                here = (middle, flux_terms(middle, own, axis + 1))
                pair = []
                for side in range(2):
                    other = [sides[2 * axis + side, part, rows, :] for part in range(5)]
                    pair.append((other, flux_terms(other, cell_terms(other), axis + 1)))
                lower, upper = face(pair[0], here), face(here, pair[1])
                step = [upper[part] - lower[part] for part in range(5)]
                change = step if change is None else [x + y for x, y in zip(change, step)]
            here = (middle, flux_terms(middle, own, 3))
            if z < 7:
                other = [state[part, z + 1, rows, :] for part in range(5)]
                upper = face(here, (other, flux_terms(other, cell_terms(other), 3)))
            else:
                upper = here[1][0]
            if z > 0:
                other = [state[part, z - 1, rows, :] for part in range(5)]
                lower = face((other, flux_terms(other, cell_terms(other), 3)), here)
                upper = [x - y for x, y in zip(upper, lower)]
            for part in range(5):
                base[part, level, rows, :] = middle[part] - STEP_RATIO * (change[part] + upper[part])
            return carry

        lax.fori_loop(0, 16, body, 0)


def exact_dot(left, right):
    return jnp.dot(left, right, precision=TOP_PRECISION, preferred_element_type=F32)


def dot_nn(left, right):
    return lax.dot_general(left, right, (((1,), (0,)), ((), ())), preferred_element_type=F32)


def dot_nt(left, right):
    return lax.dot_general(left, right, (((1,), (1,)), ((), ())), preferred_element_type=F32)


def halves(value):
    high = value.astype(BF16)
    return high, (value - high.astype(F32)).astype(BF16)


def stacked_halves(value):
    high = value.astype(BF16).astype(F32)
    return jnp.concatenate([high, value - high], axis=0).astype(BF16)


def pack_kernel(own, points, normals, support, geo, slot_row, slot_col):
    across = jnp.broadcast_to(own[...].astype(F32), (128, 128))
    along = across.T
    same = across == along
    row_rank = jnp.sum(jnp.where(same & (iota((128, 128), 0) < iota((128, 128), 1)), 1.0, 0.0), axis=0, keepdims=True)
    col_rank = jnp.sum(jnp.where(same & (iota((128, 128), 1) < iota((128, 128), 0)), 1.0, 0.0), axis=1, keepdims=True)
    slots = 2.0 * along[:1] + row_rank
    slot_row[...] = jnp.broadcast_to(slots, (8, 128))
    slot_col[...] = 2.0 * across + col_rank
    ids = jnp.concatenate([support[...].astype(F32), jnp.zeros((128, 126), F32)], axis=1)
    values = [points[:, axis, :] for axis in range(3)]
    values += [normals[:, axis, :] for axis in range(3)]
    values = jnp.concatenate(values + [ids], axis=1)
    high = values.astype(BF16)
    rest = values - high.astype(F32)
    mid = rest.astype(BF16)
    low = (rest - mid.astype(F32)).astype(BF16)
    peers = iota((128, 128), 0).astype(F32)
    for rank in range(2):
        chosen = jnp.where(slots == 2.0 * peers + rank, 1.0, 0.0).astype(BF16)
        found = dot_nn(chosen, high) + dot_nn(chosen, mid) + dot_nn(chosen, low)
        for part in range(7):
            place = (3 * rank + part, 8 + 3 * rank + part - 3, 6 + rank)[
                0 if part < 3 else 1 if part < 6 else 2
            ]
            geo[pl.ds(place, 128, stride=16), :] = found[:, part * 128 : part * 128 + 128]
    for place in (14, 15):
        geo[pl.ds(place, 128, stride=16), :] = jnp.zeros((128, 128), F32)


def table_kernel(points, table):
    row = iota((8, 128), 0)
    zero = jnp.zeros((8, 128), F32)
    for block in range(8):
        tile = points[block] - 0.5
        size = jnp.broadcast_to(jnp.sum(tile * tile, axis=0, keepdims=True), (8, 128))
        size_high = size.astype(BF16).astype(F32)
        size_mid = (size - size_high).astype(BF16).astype(F32)
        size_low = size - size_high - size_mid
        sizes = jnp.where(
            row == 0, size_high, jnp.where(row == 1, size_mid, jnp.where(row == 2, size_low, 0.0))
        )
        for rank in range(2):
            pieces = [jnp.zeros((3, 128), F32)] * 2 + [jnp.zeros((2, 128), F32)]
            pieces[rank] = -2.0 * tile
            full = jnp.concatenate(pieces, axis=0) + jnp.where(row == 6 + rank, 1.0, 0.0)
            high = full.astype(BF16).astype(F32)
            mid = (full - high).astype(BF16).astype(F32)
            low = full - high - mid
            stack = jnp.concatenate(
                [high, mid, low, high, mid, high, sizes, zero] + [zero] * 8, axis=0
            )
            table[rank * 8 + block] = stack.T[:, :64].astype(BF16)


def spread_field(field, wide):
    for block in range(8):
        wide[block] = stacked_halves(field[pl.ds(block * 8, 8), :])


def moved_row(wide, tile, blocks, normal):
    left = jnp.concatenate([wide[block] for block in blocks], axis=1)
    moved = dot_nn(left, tile)
    moved = moved[:, :128] + moved[:, 128:]
    moved = moved[:3] + moved[8:11]
    return jnp.sum(moved * normal, axis=0, keepdims=True)


def tile_copy(source, target, sems, step):
    part = pl.ds(pl.multiple_of(step * 2 * PEERS, 2 * PEERS), 2 * PEERS)
    return pltpu.make_async_copy(source.at[part], target.at[part], sems.at[step])


def fetch_tiles(phi_hbm, phi, sems):
    def begin(step, carry):
        tile_copy(phi_hbm, phi, sems, step).start()
        return carry

    lax.fori_loop(0, STEPS, begin, 0)


def phi_kernel(support, geo, table, field, phi_hbm, motion, wide, phi, sems):
    spread_field(field, wide)
    row = iota((8, 128), 0)

    def body(step, carry):
        rows = []
        for peer in range(PEERS):
            start = pl.multiple_of((step * PEERS + peer) * 16, 16)
            tile = geo[pl.ds(start, 8), :] - 0.5
            normals = geo[pl.ds(start + 8, 8), :]
            square = tile * tile
            first = jnp.sum(jnp.where(row < 3, square, 0.0), axis=0, keepdims=True)
            second = jnp.sum(jnp.where((row >= 3) & (row < 6), square, 0.0), axis=0, keepdims=True)
            places = jnp.where(row < 6, tile, jnp.where(row == 6, first, second))
            high = places.astype(BF16).astype(F32)
            mid = (places - high).astype(BF16).astype(F32)
            low = places - high - mid
            ones = jnp.ones((8, 128), F32)
            right = jnp.concatenate(
                [high, high, high, mid, mid, low, ones, jnp.zeros((8, 128), F32)], axis=0
            ).astype(BF16)
            for rank in range(2):
                slot = (step * PEERS + peer) * 2 + rank
                tiles, blocks = [], []
                for k in range(2):
                    block = support[slot * 2 + k]
                    squared = jnp.maximum(dot_nn(table[rank * 8 + block], right), 1e-30)
                    ratio = squared * lax.rsqrt(squared)
                    reach = jnp.maximum(1.0 - ratio, 0.0)
                    reach = reach * reach
                    value = reach * reach * (4.0 * ratio + 1.0)
                    tiles.append(jnp.concatenate(halves(value), axis=1))
                    blocks.append(block)
                tile = jnp.concatenate(tiles, axis=0)
                phi[slot] = tile
                rows.append(moved_row(wide, tile, blocks, normals[3 * rank : 3 * rank + 3]))
        motion[pl.ds(pl.multiple_of(step * 2 * PEERS, 8), 8), :] = jnp.concatenate(rows, axis=0)
        tile_copy(phi, phi_hbm, sems, step).start()
        return carry

    lax.fori_loop(0, STEPS, body, 0)

    def finish(step, carry):
        tile_copy(phi, phi_hbm, sems, step).wait()
        return carry

    lax.fori_loop(0, STEPS, finish, 0)


def motion_kernel(support, geo, field, phi_hbm, motion, wide, phi, sems):
    fetch_tiles(phi_hbm, phi, sems)
    spread_field(field, wide)

    def body(step, carry):
        tile_copy(phi_hbm, phi, sems, step).wait()
        rows = []
        for index in range(2 * PEERS):
            slot = step * PEERS * 2 + index
            rank = index % 2
            start = pl.multiple_of((step * PEERS + index // 2) * 16, 16)
            normals = geo[pl.ds(start + 8, 8), :]
            blocks = [support[slot * 2 + k] for k in range(2)]
            rows.append(moved_row(wide, phi[slot], blocks, normals[3 * rank : 3 * rank + 3]))
        motion[pl.ds(pl.multiple_of(step * 2 * PEERS, 8), 8), :] = jnp.concatenate(rows, axis=0)
        return carry

    lax.fori_loop(0, STEPS, body, 0)


def wall_kernel(received, slot_row, slot_col, bottom, base, fresh, sent):
    lanes = iota((128, 256), 1).astype(F32)
    column = jnp.concatenate([slot_col[...], slot_col[...]], axis=1)
    argument = exact_dot(jnp.where(column == lanes, 1.0, 0.0), received[...])
    wall = WALL_SPEED * jnp.tanh(WALL_GAIN * argument)
    lower = [bottom[part] for part in range(5)]
    ghost = [lower[0], lower[1], lower[2], 2.0 * lower[0] * wall - lower[3], lower[4]]
    inverse = 1.0 / lower[0]

    def terms(state):
        velocity = state[3] * inverse
        pressure = 0.4 * (
            state[4]
            - 0.5 * (state[1] * state[1] + state[2] * state[2] + state[3] * state[3]) * inverse
        )
        flux = [part * velocity for part in state]
        flux[3] = flux[3] + pressure
        flux[4] = flux[4] + pressure * velocity
        return flux, jnp.abs(velocity) + jnp.sqrt(1.4 * pressure * inverse)

    ghost_flux, ghost_speed = terms(ghost)
    lower_flux, lower_speed = terms(lower)
    speed = jnp.maximum(ghost_speed, lower_speed)
    new = []
    for part in range(5):
        face = 0.5 * (ghost_flux[part] + lower_flux[part])
        if part == 3:
            face = face - 0.5 * speed * (lower[3] - ghost[3])
        new.append(base[part] + STEP_RATIO * face)
        fresh[part] = new[part]
    pressure = 0.4 * (
        new[4] - 0.5 * (new[1] * new[1] + new[2] * new[2] + new[3] * new[3]) / new[0]
    )
    amount = -LOAD_SCALE * (pressure - PRESSURE_REF)
    chosen = jnp.where(slot_row[:1] == iota((256, 128), 0).astype(F32), 1.0, 0.0)
    sent[...] = exact_dot(chosen, amount)


def spread_back(values, couplings, pattern, total):
    total[...] = jnp.zeros((64, 128), F32)

    def body(block, carry):
        stack = stacked_halves(values[pl.ds(pl.multiple_of(block * 8, 8), 8), :])
        for k in range(4):
            upper, lower = halves(couplings[block, k])
            term = dot_nn(stack, upper) + dot_nn(stack, lower)
            place = pl.ds(pl.multiple_of(pattern[block * 4 + k] * 8, 8), 8)
            total[place, :] = total[place, :] + term[:8] + term[8:]
        return carry

    lax.fori_loop(0, 8, body, 0)


def gather_forward(values, couplings, pattern, total):
    def body(block, carry):
        term = jnp.zeros((16, 128), F32)
        for k in range(4):
            place = pl.ds(pl.multiple_of(pattern[block * 4 + k] * 8, 8), 8)
            stack = stacked_halves(values[place, :])
            upper, lower = halves(couplings[block, k])
            term = term + dot_nt(stack, upper) + dot_nt(stack, lower)
        total[pl.ds(pl.multiple_of(block * 8, 8), 8), :] = term[:8] + term[8:]
        return carry

    lax.fori_loop(0, 8, body, 0)


def back_kernel(pattern, values, couplings, total):
    spread_back(values, couplings, pattern, total)


def loads_kernel(
    support, pattern, amounts, geo, phi_hbm, base, couplings, start, back, loads, phi, sems
):
    fetch_tiles(phi_hbm, phi, sems)
    loads[...] = jnp.zeros((8, 8, 128), F32)
    row = iota((8, 128), 0)

    def body(step, carry):
        tile_copy(phi_hbm, phi, sems, step).wait()
        forces = amounts[pl.ds(pl.multiple_of(step * 2 * PEERS, 8), 8), :]
        for peer in range(PEERS):
            place = pl.multiple_of((step * PEERS + peer) * 16, 16)
            tile = geo[pl.ds(place + 8, 8), :]
            for rank in range(2):
                index = peer * 2 + rank
                slot = step * PEERS * 2 + index
                kept = (row >= 3 * rank) & (row < 3 * rank + 3)
                stack = stacked_halves(jnp.where(kept, tile * forces[index : index + 1], 0.0))
                stack = jnp.concatenate([stack, stack], axis=1)
                term = dot_nt(stack, phi[slot])
                term = term[:8] + term[8:]
                for k in range(2):
                    block = support[slot * 2 + k]
                    loads[block] = loads[block] + term[:, k * 128 : k * 128 + 128]
        return carry

    lax.fori_loop(0, STEPS, body, 0)
    for block in range(8):
        tile = loads[block]
        start[pl.ds(block * 8, 8), :] = base[pl.ds(block * 8, 8), :] + jnp.where(
            row < 3, tile + pltpu.roll(tile, 5, 0), 0.0
        )
    spread_back(start, couplings, pattern, back)


def apply_kernel(shift, pattern, values, before, behind, diagonal, couplings, image, work):
    gather_forward(before, couplings, pattern, work)
    image[...] = (diagonal[...] - shift) * values[...] - (1.0 / 1024.0) * (
        work[...] + behind[...]
    )


def row_sum(value):
    return jnp.sum(value, axis=0, keepdims=True)


def sums_kernel(
    pattern, start, image, before, diagonal, couplings, tested, extra, own, row, work, stack
):
    gather_forward(before, couplings, pattern, work)
    first, second = start[...], image[...]
    stack[...] = jnp.zeros((128, 128), F32)
    for h in range(8):
        stack[pl.ds(h, 1), :] = row_sum(tested[h] * first)
        stack[pl.ds(8 + h, 1), :] = row_sum(tested[h] * second)
    third = second * ((diagonal[...] - SHIFT) * second - (2.0 / 1024.0) * work[...])
    stack[pl.ds(16, 1), :] = row_sum(first * first)
    stack[pl.ds(17, 1), :] = row_sum(first * second)
    stack[pl.ds(18, 1), :] = row_sum(second * second)
    stack[pl.ds(19, 1), :] = row_sum(third)
    stack[pl.ds(20, 1), :] = row_sum(extra[...] * first)
    stack[pl.ds(21, 1), :] = row_sum(extra[...] * second)
    sums = jnp.sum(stack[...], axis=1, keepdims=True)
    row[...] = jnp.broadcast_to(sums, (128, 128)).T + own[...]


def solve_kernel(
    count, received, memory, field, start, image, last, responses, estimate, residual, *more
):
    totals = row_sum(received[...])

    def lane(index):
        return totals[:, index : index + 1]

    lanes, row = iota((8, 128), 1), iota((8, 128), 0)

    def column(values):
        return jnp.sum(
            jnp.where(lanes == row, jnp.broadcast_to(values, (8, 128)), 0.0), axis=1, keepdims=True
        )

    m0, m1, m2, m3 = lane(16), lane(17), lane(18), lane(19)
    alpha = m0 / (m1 + SHIFT * m0)
    gain = 1.0 - alpha * SHIFT
    norm = gain * gain * m0 - 2.0 * gain * alpha * m1 + alpha * alpha * m2
    mix = gain + norm / m0
    curve = (
        mix * mix * (m1 + SHIFT * m0)
        - 2.0 * mix * alpha * (m2 + SHIFT * m1)
        + alpha * alpha * (m3 + SHIFT * m2)
    )
    follow = norm / curve
    c0 = alpha + follow * mix
    c1 = -follow * alpha
    change = c0 * start[...] + c1 * image[...]
    response = field[...] + change
    size = c0 * c0 * m0 + 2.0 * c0 * c1 * m1 + c1 * c1 * m2
    projected = c0 * totals + c1 * pltpu.roll(totals, 120, 1)
    lane_row = iota((1, 128), 1)
    if count == 0:
        picked = jnp.where(
            (lanes >= 64 + 8 * row) & (lanes < 72 + 8 * row),
            jnp.broadcast_to(totals, (8, 128)),
            0.0,
        )
        fold = jnp.where(
            (iota((128, 128), 0) >= 64) & (iota((128, 128), 0) % 8 == iota((128, 128), 1)), 1.0, 0.0
        )
        gram = exact_dot(picked, fold)
    else:
        overlap = c0 * lane(20) + c1 * lane(21)
        newest = size - overlap
        edge = projected - memory[8:9, :]
        edge = jnp.where(lane_row == 0, newest - overlap + memory[9:10, :1], edge)
        projected = jnp.where(lane_row == 0, newest, projected)
        gram = jnp.where(
            row == 0, jnp.broadcast_to(edge, (8, 128)), jnp.where(lanes == 0, column(edge), memory[:8, :])
        )
    system = jnp.where(lanes < 8, gram, jnp.where(lanes == 8, column(projected), 0.0))
    for j in range(8):
        pivot = system[j : j + 1] / system[j : j + 1, j : j + 1]
        system = jnp.where(row == j, pivot, system - system[:, j : j + 1] * pivot)
    result = response
    for h in range(8):
        weight = system[h : h + 1, 8:9]
        used = responses[h] if count == 0 or h > 0 else response - last[...]
        result = result - weight * used
    if count == 0:
        kept, saved = more
        estimate[...] = result
        residual[...] = change
        kept[...] = response
        saved[:8, :] = gram
        saved[8:16, :] = jnp.where(
            row == 0, jnp.broadcast_to(projected, (8, 128)), jnp.where(row == 1, size, 0.0)
        )
    else:
        for block in range(8):
            estimate[block] = result[block * 8 : block * 8 + 3]
            residual[block] = change[block * 8 : block * 8 + 3]


def shape(*dims, dtype=F32):
    return jax.ShapeDtypeStruct(dims, dtype)


def call(kernel, outs, scratch=(), scalars=0, cost=None, **kw):
    specs = [pl.BlockSpec(memory_space=SMEM)] * scalars

    def run(*args):
        return pl.pallas_call(
            kernel,
            out_shape=outs,
            in_specs=specs + [pl.BlockSpec()] * (len(args) - scalars),
            out_specs=jax.tree.map(lambda _: pl.BlockSpec(), outs),
            scratch_shapes=list(scratch),
            compiler_params=pltpu.CompilerParams(vmem_limit_bytes=14 << 20),
            cost_estimate=cost,
            **kw,
        )(*args)

    return run


def exchange(values):
    return lax.all_to_all(values, AXES, split_axis=0, concat_axis=0, tiled=True)


def forward(values):
    return lax.ppermute(values, AXES, [(i, (i + 1) % DEVICES) for i in range(DEVICES)])


def backward(values):
    return lax.ppermute(values, AXES, [((i + 1) % DEVICES, i) for i in range(DEVICES)])


def shift(values, axis, step):
    count = lax.axis_size(axis)
    return lax.ppermute(values, axis, [(i, (i + step) % count) for i in range(count)])


STEPS = DEVICES // PEERS
WIDE = pltpu.VMEM((8, 16, 128), BF16)
PHI_COST = pl.CostEstimate(flops=2_000_000_000, bytes_accessed=40_000_000, transcendentals=0)
RESIDENT = pl.BlockSpec(memory_space=pl.ANY)
HELD = [pltpu.VMEM((256, 256, 256), BF16), pltpu.SemaphoreType.DMA((DEVICES // PEERS,))]


def whole(kernel, scalars, in_specs, out_specs, outs, scratch, args):
    return pl.pallas_call(
        kernel,
        out_shape=outs,
        in_specs=[pl.BlockSpec(memory_space=SMEM)] * scalars + in_specs,
        out_specs=out_specs,
        scratch_shapes=scratch,
        compiler_params=pltpu.CompilerParams(vmem_limit_bytes=56 << 20),
        cost_estimate=PHI_COST,
    )(*args)


def build_phi(support, geo, table, field):
    return whole(
        phi_kernel,
        1,
        [pl.BlockSpec()] * 3,
        [RESIDENT, pl.BlockSpec()],
        [shape(256, 256, 256, dtype=BF16), shape(256, 128)],
        [WIDE] + HELD,
        (support, geo, table, field),
    )


def find_motion(support, geo, field, phi):
    return whole(
        motion_kernel,
        1,
        [pl.BlockSpec()] * 2 + [RESIDENT],
        pl.BlockSpec(),
        shape(256, 128),
        [WIDE] + HELD,
        (support, geo, field, phi),
    )


def find_loads(support, pattern, amounts, geo, phi, base, couplings):
    return whole(
        loads_kernel,
        2,
        [pl.BlockSpec()] * 2 + [RESIDENT] + [pl.BlockSpec()] * 2,
        [pl.BlockSpec(), pl.BlockSpec()],
        [shape(64, 128), shape(64, 128)],
        [pltpu.VMEM((8, 8, 128), F32)] + HELD,
        (support, pattern, amounts, geo, phi, base, couplings),
    )


def padded(values):
    wide = [(0, 0)] * (values.ndim - 2) + [(0, 5), (0, 0)]
    values = jnp.pad(values, wide)
    return values.reshape(values.shape[:-3] + (64, 128))


def on_device(
    fluid_state,
    surface_points,
    surface_normals,
    owner_ids,
    support_ids,
    struct_points,
    couplings,
    coupling_pattern,
    stiff_diagonal,
    struct_load,
    predicted,
    hist_residual,
    hist_response,
):
    pattern = coupling_pattern.reshape(32)
    geo, slot_row, slot_col = call(
        pack_kernel, [shape(2048, 128), shape(8, 128), shape(128, 128)]
    )(owner_ids, surface_points, surface_normals, support_ids)
    geo = exchange(geo)
    support = geo.reshape(128, 16, 128)[:, 6:8, :2].astype(jnp.int32).reshape(512)
    low_x, high_x, low_y, high_y = call(edges_kernel, [shape(40, 128)] * 4)(fluid_state)
    sides = [
        shift(low_x, "fx", -1),
        shift(high_x, "fx", 1),
        shift(low_y, "fy", -1),
        shift(high_y, "fy", 1),
    ]
    diagonal = padded(jnp.broadcast_to(stiff_diagonal[:, None, :], (8, 3, 128)))
    load = padded(struct_load)
    field = padded(predicted)
    tested = padded(hist_residual)
    responses = padded(hist_response)
    own = jnp.pad(
        jnp.einsum("hbdp,gbdp->hg", hist_residual, hist_residual, precision=TOP_PRECISION).reshape(
            1, 64
        ),
        ((0, 0), (64, 0)),
    )
    table = call(table_kernel, shape(16, 128, 64, dtype=BF16))(struct_points)

    def back_of(values):
        return call(back_kernel, shape(64, 128), scalars=1)(pattern, values, couplings)

    def applied(values, back, shift, gate=None):
        before, behind = forward(values), backward(back)
        if gate is not None:
            before, behind, _ = lax.optimization_barrier((before, behind, gate))
        return call(
            functools.partial(apply_kernel, shift),
            shape(64, 128),
            [pltpu.VMEM((64, 128), F32)],
            scalars=1,
        )(pattern, values, before, behind, diagonal, couplings)

    phi, motion = build_phi(support, geo, table, field)
    halos, motion = lax.optimization_barrier(
        ((sides[1], sides[0], sides[3], sides[2]), motion)
    )

    def fluid(levels, gate=None):
        ends = halos
        if gate is not None:
            ends, _ = lax.optimization_barrier((halos, gate))
        return call(
            functools.partial(fluid_kernel, levels),
            shape(5, len(levels), 128, 128),
            [pltpu.VMEM((4, 5, 128, 128), F32)],
            cost=pl.CostEstimate(
                flops=len(levels) * 40_000_000, bytes_accessed=len(levels) * 700_000, transcendentals=0
            ),
        )(fluid_state, *ends)

    bottom = fluid_state[:, 0]
    base_bottom = fluid((0,)).reshape(5, 128, 128)
    fluid_parts = []
    extra = field
    memory = diagonal
    last = field
    for count in range(2):
        if count > 0:
            motion = find_motion(support, geo, field, phi)
        received = exchange(motion)
        fresh, sent = call(wall_kernel, [shape(5, 128, 128), shape(256, 128)])(
            received, slot_row, slot_col, bottom, base_bottom
        )
        amounts = exchange(sent)
        base = load - applied(field, back_of(field), 0.0, sent)
        fluid_parts.append(fluid((1, 2, 3) if count == 0 else (6, 7), sent))
        amounts, fluid_parts[-1] = lax.optimization_barrier((amounts, fluid_parts[-1]))
        start, back = find_loads(support, pattern, amounts, geo, phi, base, couplings)
        image = applied(start, back, SHIFT)
        row = call(
            sums_kernel,
            shape(128, 128),
            [pltpu.VMEM((64, 128), F32), pltpu.VMEM((128, 128), F32)],
            scalars=1,
        )(
            pattern,
            start,
            image,
            forward(image),
            diagonal,
            couplings,
            tested,
            extra,
            own if count == 0 else jnp.zeros_like(own),
        )
        totals = exchange(row)
        if count == 0:
            fluid_parts.append(fluid((4, 5), row))
            totals, fluid_parts[-1] = lax.optimization_barrier((totals, fluid_parts[-1]))
        solve = functools.partial(solve_kernel, count)
        if count == 0:
            outs = [shape(64, 128), shape(64, 128), shape(64, 128), shape(16, 128)]
            field, extra, last, memory = call(solve, outs)(
                totals, jnp.zeros((16, 128), F32), field, start, image, last, responses
            )
        else:
            outs = [shape(8, 3, 128), shape(8, 3, 128)]
            estimate, residual = call(solve, outs)(
                totals, memory, field, start, image, last, responses
            )
    new_state = jnp.concatenate([fresh[:, None]] + fluid_parts, axis=1)
    return (new_state, estimate, residual)


def solution(mesh):
    placed = (
        P(None, None, "fx", "fy"),
        P(("fx", "fy"), None, None),
        P(("fx", "fy"), None, None),
        P(("fx", "fy"), None),
        P(("fx", "fy"), None),
        P(("fx", "fy"), None, None),
        P(("fx", "fy"), None, None, None),
        P(("fx", "fy"), None),
        P(("fx", "fy"), None),
        P(("fx", "fy"), None, None),
        P(("fx", "fy"), None, None),
        P(None, ("fx", "fy"), None, None),
        P(None, ("fx", "fy"), None, None),
    )
    return jax.shard_map(
        on_device,
        mesh=mesh,
        in_specs=placed,
        out_specs=(
            P(None, None, "fx", "fy"),
            P(("fx", "fy"), None, None),
            P(("fx", "fy"), None, None),
        ),
        check_vma=False,
    )
```

profile of v0, /device:TPU:1, one launch (start us, length us, event | category | flops | bytes accessed | tf_op | source)
XLA Modules:
  0.0 287.7 jit_solution(18014242443269273989)
XLA Ops:
  4.3 1.9 shard_map.148
  6.3 12.0 %all-to-all-start = ((f32[128,16,128]{2,1,0:T(8,128)}), f32[128,16,128]{2,1,0:T(8,128)}, u32[]{:S(2)}, u32[]{:S(2)}) async-start(f32[128,16,128]{2,1,0:T(8,128)} %bitcast), calls=%async_computation | async-start | bytes 2097152 | tf_op jit(solution)/shard_map/all_to_all | solution.py:531
  18.2 1.7 copy-done.3
  20.0 1.7 shard_map.149
  21.7 1.6 collective-permute-start
  23.3 4.0 %collective-permute-start.1 = (f32[40,128]{1,0:T(8,128)S(1)}, f32[40,128]{1,0:T(8,128)S(1)}, u32[]{:S(2)}, u32[]{:S(2)}) collective-permute-start(f32[40,128]{1,0:T(8,128)S(1)} %get-tuple-element.54), channel_id=1, source_target_pairs={{0,120},{8,0},{16,8},{24,16},{32,24},{40,32},{48,40},{56,48},{64,5... | collective-permute-start | bytes 61448 | tf_op jit(solution)/shard_map/ppermute | solution.py:544
  27.3 1.8 collective-permute-start.2
  29.7 1.7 collective-permute-start.4
  32.6 2.9 %shard_map.155 = f32[64,128]{1,0:T(8,128)} custom-call(s32[32]{0:T(128)S(1)} %reshape.51.pattern, f32[64,128]{1,0:T(8,128)} %pad_bitcast_fusion.3.field.values.extra.last, f32[8,4,128,128]{3,2,1,0:T(8,128)S(1)} %copy-done), custom_call_target="tpu_custom_call" | custom-call | tf_op jit(solution)/shard_map/pallas_call | solution.py:516
  35.5 1.6 all-to-all-done
  39.0 28.6 %shard_map.151 = (bf16[256,256,256]{2,1,0:T(8,128)(2,1)}, f32[256,128]{1,0:T(8,128)}) custom-call(s32[512]{0:T(512)} %reshape.50.support, f32[2048,128]{1,0:T(8,128)} %bitcast.1.geo, bf16[16,128,64]{2,1,0:T(8,128)(2,1)} %copy-done.18, f32[64,128]{1,0:T(8,128)} %pad_bitcast_fusion.3.field.values.extra.last), custom_call_target="tpu_custom_call" | custom-call | flops 2000000000 | bytes 40000000 | tf_op jit(solution)/shard_map/pallas_call | solution.py:555
  68.8 8.4 %all-to-all-start.1 = ((f32[128,2,128]{2,1,0:T(2,128)}), f32[128,2,128]{2,1,0:T(2,128)S(1)}, u32[]{:S(2)}, u32[]{:S(2)}) async-start(f32[128,2,128]{2,1,0:T(2,128)} %bitcast.53), calls=%async_computation.1 | async-start | bytes 262144 | tf_op jit(solution)/shard_map/all_to_all | solution.py:531
  79.0 1.7 copy-done.4
  82.2 5.1 %all-to-all-done.1 = f32[128,2,128]{2,1,0:T(2,128)S(1)} async-done(((f32[128,2,128]{2,1,0:T(2,128)}), f32[128,2,128]{2,1,0:T(2,128)S(1)}, u32[]{:S(2)}, u32[]{:S(2)}) %all-to-all-start.1) | async-done | bytes 131104 | tf_op jit(solution)/shard_map/all_to_all | solution.py:531
  87.3 1.5 shard_map.153
  88.8 5.3 %all-to-all-start.2 = ((f32[128,2,128]{2,1,0:T(2,128)}), f32[128,2,128]{2,1,0:T(2,128)}, u32[]{:S(2)}, u32[]{:S(2)}) async-start(f32[128,2,128]{2,1,0:T(2,128)} %bitcast.7), calls=%async_computation.2 | async-start | bytes 262144 | tf_op jit(solution)/shard_map/all_to_all | solution.py:531
  94.1 2.9 shard_map.156
  97.0 1.7 copy-done.5
  98.7 4.8 %shard_map.154 = f32[5,3,128,128]{3,2,1,0:T(8,128)S(1)} custom-call(f32[5,8,128,128]{3,2,1,0:T(8,128)S(1)} %copy-done.5, f32[40,128]{1,0:T(8,128)S(1)} %collective-permute-done.low_x, f32[40,128]{1,0:T(8,128)S(1)} %collective-permute-done.1.high_x, f32[40,128]{1,0:T(8,128)S(1)} %collective-permute-done.2.low_y, f32[40,128]{1,0:T(8,128)S(1)} %collective-permute-done.3.high_y), custom_call_target="tpu_custom_call" | custom-call | flops 120000000 | bytes 2100000 | tf_op jit(solution)/shard_map/pallas_call | solution.py:516
  104.2 18.9 %shard_map.157 = (f32[64,128]{1,0:T(8,128)}, f32[64,128]{1,0:T(8,128)}) custom-call(s32[512]{0:T(512)} %reshape.50.support, s32[32]{0:T(128)} %copy-done.28, f32[256,128]{1,0:T(8,128)} %bitcast.8.amounts, f32[2048,128]{1,0:T(8,128)} %bitcast.1.geo, bf16[256,256,256]{2,1,0:T(8,128)(2,1)} %get-tuple-element.71.phi_hbm, f32[64,128]{1,0:T(8,128)} %fusion.2.base, ...), custom_call_target="tpu_custom_call" | custom-call | flops 2000000000 | bytes 40000000 | tf_op jit(solution)/shard_map/pallas_call | solution.py:555
  123.1 1.7 collective-permute-start.6
  126.1 2.2 collective-permute-done.7.behind
  129.1 3.2 %shard_map.158.image = f32[64,128]{1,0:T(8,128)} custom-call(s32[32]{0:T(128)S(1)} %copy-done.29, f32[64,128]{1,0:T(8,128)S(1)} %copy-done.23, f32[64,128]{1,0:T(8,128)S(1)} %collective-permute-done.6.before, f32[64,128]{1,0:T(8,128)S(1)} %collective-permute-done.7.behind, f32[64,128]{1,0:T(8,128)S(1)} %pad_bitcast_fusion.4.diagonal, ...), custom_call_target="tpu_custom_call" | custom-call | tf_op jit(solution)/shard_map/pallas_call | solution.py:516
  134.7 1.6 copy.71
  140.0 3.1 %shard_map.159 = f32[128,128]{1,0:T(8,128)S(1)} custom-call(s32[32]{0:T(128)S(1)} %copy-done.30, f32[64,128]{1,0:T(8,128)S(1)} %copy-done.23, f32[64,128]{1,0:T(8,128)} %shard_map.158.image, f32[64,128]{1,0:T(8,128)} %collective-permute-done.8.before, f32[64,128]{1,0:T(8,128)S(1)} %pad_bitcast_fusion.4.diagonal, f32[8,4,128,128]{3,2,1,0:T(8,128)S(1)} %copy-done.1, ...), custom_call_target="tpu_custom_call" | custom-call | tf_op jit(solution)/shard_map/pallas_call | solution.py:516
  143.8 12.4 %all-to-all-start.3 = ((f32[128,1,128]{2,1,0:T(1,128)}), f32[128,1,128]{2,1,0:T(1,128)}, u32[]{:S(2)}, u32[]{:S(2)}) async-start(f32[128,1,128]{2,1,0:T(1,128)} %bitcast.49), calls=%async_computation.3 | async-start | bytes 131072 | tf_op jit(solution)/shard_map/all_to_all | solution.py:531
  156.1 1.6 pad_bitcast_fusion.responses
  157.8 1.7 copy-done.6
  159.5 3.2 %shard_map.160 = f32[5,2,128,128]{3,2,1,0:T(8,128)S(1)} custom-call(f32[5,8,128,128]{3,2,1,0:T(8,128)S(1)} %copy-done.6, f32[40,128]{1,0:T(8,128)S(1)} %collective-permute-done.low_x, f32[40,128]{1,0:T(8,128)S(1)} %collective-permute-done.1.high_x, f32[40,128]{1,0:T(8,128)S(1)} %collective-permute-done.2.low_y, f32[40,128]{1,0:T(8,128)S(1)} %collective-permute-done.3.high_y), custom_call_target="tpu_custom_call" | custom-call | flops 80000000 | bytes 1400000 | tf_op jit(solution)/shard_map/pallas_call | solution.py:516
  163.6 1.9 all-to-all-done.3
  166.4 2.0 shard_map.161
  170.8 13.0 %shard_map.162 = f32[256,128]{1,0:T(8,128)} custom-call(s32[512]{0:T(512)} %reshape.50.support, f32[2048,128]{1,0:T(8,128)} %bitcast.1.geo, f32[64,128]{1,0:T(8,128)} %copy-done.16, bf16[256,256,256]{2,1,0:T(8,128)(2,1)} %get-tuple-element.71.phi_hbm), custom_call_target="tpu_custom_call" | custom-call | flops 2000000000 | bytes 40000000 | tf_op jit(solution)/shard_map/pallas_call | solution.py:555
  183.9 8.4 %all-to-all-start.4 = ((f32[128,2,128]{2,1,0:T(2,128)}), f32[128,2,128]{2,1,0:T(2,128)}, u32[]{:S(2)}, u32[]{:S(2)}) async-start(f32[128,2,128]{2,1,0:T(2,128)} %bitcast.52), calls=%async_computation.4 | async-start | bytes 262144 | tf_op jit(solution)/shard_map/all_to_all | solution.py:531
  193.0 2.7 shard_map.165
  197.4 4.6 %all-to-all-done.4 = f32[128,2,128]{2,1,0:T(2,128)} async-done(((f32[128,2,128]{2,1,0:T(2,128)}), f32[128,2,128]{2,1,0:T(2,128)}, u32[]{:S(2)}, u32[]{:S(2)}) %all-to-all-start.4) | async-done | bytes 131104 | tf_op jit(solution)/shard_map/all_to_all | solution.py:531
  204.5 1.7 shard_map.163
  207.7 9.8 %all-to-all-start.5 = ((f32[128,2,128]{2,1,0:T(2,128)}), f32[128,2,128]{2,1,0:T(2,128)S(1)}, u32[]{:S(2)}, u32[]{:S(2)}) async-start(f32[128,2,128]{2,1,0:T(2,128)} %bitcast.50), calls=%async_computation.5 | async-start | bytes 262144 | tf_op jit(solution)/shard_map/all_to_all | solution.py:531
  218.2 2.9 shard_map.166
  221.0 1.7 copy-done.7
  222.8 3.1 %shard_map.164 = f32[5,2,128,128]{3,2,1,0:T(8,128)S(1)} custom-call(f32[5,8,128,128]{3,2,1,0:T(8,128)S(1)} %copy-done.7, f32[40,128]{1,0:T(8,128)S(1)} %collective-permute-done.low_x, f32[40,128]{1,0:T(8,128)S(1)} %collective-permute-done.1.high_x, f32[40,128]{1,0:T(8,128)S(1)} %collective-permute-done.2.low_y, f32[40,128]{1,0:T(8,128)S(1)} %collective-permute-done.3.high_y), custom_call_target="tpu_custom_call" | custom-call | flops 80000000 | bytes 1400000 | tf_op jit(solution)/shard_map/pallas_call | solution.py:516
  228.1 18.9 %shard_map.167 = (f32[64,128]{1,0:T(8,128)}, f32[64,128]{1,0:T(8,128)}) custom-call(s32[512]{0:T(512)} %reshape.50.support, s32[32]{0:T(128)} %copy-done.28, f32[256,128]{1,0:T(8,128)} %bitcast.51, f32[2048,128]{1,0:T(8,128)} %bitcast.1.geo, bf16[256,256,256]{2,1,0:T(8,128)(2,1)} %get-tuple-element.71.phi_hbm, f32[64,128]{1,0:T(8,128)} %fusion.1.base, ...), custom_call_target="tpu_custom_call" | custom-call | flops 2000000000 | bytes 40000000 | tf_op jit(solution)/shard_map/pallas_call | solution.py:555
  249.1 2.2 collective-permute-done.12.behind
  252.1 2.6 shard_map.168.image
  254.9 6.0 %collective-permute-done.13.before = f32[64,128]{1,0:T(8,128)S(1)} collective-permute-done((f32[64,128]{1,0:T(8,128)S(1)}, f32[64,128]{1,0:T(8,128)S(1)}, u32[]{:S(2)}, u32[]{:S(2)}) %collective-permute-start.13) | collective-permute-done | bytes 32800 | tf_op jit(solution)/shard_map/ppermute | solution.py:535
  260.8 3.5 %shard_map.169 = f32[128,128]{1,0:T(8,128)} custom-call(s32[32]{0:T(128)S(1)} %copy-done.33, f32[64,128]{1,0:T(8,128)S(1)} %copy-done.21, f32[64,128]{1,0:T(8,128)S(1)} %shard_map.168.image, f32[64,128]{1,0:T(8,128)S(1)} %collective-permute-done.13.before, f32[64,128]{1,0:T(8,128)S(1)} %pad_bitcast_fusion.4.diagonal, f32[8,4,128,128]{3,2,1,0:T(8,128)S(1)} %copy-done.2, ...), custom_call_target="tpu_custom_call" | custom-call | tf_op jit(solution)/shard_map/pallas_call | solution.py:516
  264.3 11.4 %all-to-all-start.6 = ((f32[128,1,128]{2,1,0:T(1,128)}), f32[128,1,128]{2,1,0:T(1,128)S(1)}, u32[]{:S(2)}, u32[]{:S(2)}) async-start(f32[128,1,128]{2,1,0:T(1,128)} %bitcast.25), calls=%async_computation.6 | async-start | bytes 131072 | tf_op jit(solution)/shard_map/all_to_all | solution.py:531
  275.8 1.8 pad_maximum_fusion
  277.6 7.8 %all-to-all-done.6 = f32[128,1,128]{2,1,0:T(1,128)S(1)} async-done(((f32[128,1,128]{2,1,0:T(1,128)}), f32[128,1,128]{2,1,0:T(1,128)S(1)}, u32[]{:S(2)}, u32[]{:S(2)}) %all-to-all-start.6) | async-done | bytes 65568 | tf_op jit(solution)/shard_map/all_to_all | solution.py:531
  (152 shorter events, 40.0 us)
Async XLA Ops:
  4.3 24.7 %copy-start.48 = (f32[8,3,128]{2,0,1:T(8,128)S(1)}, f32[8,3,128]{2,0,1:T(8,128)}, u32[]{:S(2)}) copy-start(f32[8,3,128]{2,0,1:T(8,128)} %param.23) | copy-start | bytes 36868
  4.3 27.1 %copy-start.49 = (f32[8,3,128]{2,0,1:T(8,128)S(1)}, f32[8,3,128]{2,0,1:T(8,128)}, u32[]{:S(2)}) copy-start(f32[8,3,128]{2,0,1:T(8,128)} %param.18) | copy-start | bytes 36868
  6.3 81.0 %copy-start.25 = (f32[128,128]{1,0:T(8,128)}, f32[128,128]{1,0:T(8,128)S(1)}, u32[]{:S(2)}) copy-start(f32[128,128]{1,0:T(8,128)S(1)} %get-tuple-element.60.slot_col) | copy-start | bytes 196612
  6.3 81.0 %copy-start.38 = (f32[8,128]{1,0:T(8,128)}, f32[8,128]{1,0:T(8,128)S(1)}, u32[]{:S(2)}) copy-start(f32[8,128]{1,0:T(8,128)S(1)} %get-tuple-element.59.slot_row) | copy-start | bytes 12292
  6.3 26.3 %copy-start = (f32[8,4,128,128]{3,2,1,0:T(8,128)S(1)}, f32[8,4,128,128]{3,2,1,0:T(8,128)}, u32[]{:S(2)}) copy-start(f32[8,4,128,128]{3,2,1,0:T(8,128)} %couplings.19) | copy-start | bytes 6291460
  6.3 30.8 %all-to-all-start = ((f32[128,16,128]{2,1,0:T(8,128)}), f32[128,16,128]{2,1,0:T(8,128)}, u32[]{:S(2)}, u32[]{:S(2)}) async-start(f32[128,16,128]{2,1,0:T(8,128)} %bitcast), calls=%async_computation | async-start | bytes 2097152 | tf_op jit(solution)/shard_map/all_to_all | solution.py:531
  20.0 12.5 %copy-start.52 = (s32[8,4]{0,1:T(4,128)S(1)}, s32[8,4]{0,1:T(4,128)}, u32[]{:S(2)}) copy-start(s32[8,4]{0,1:T(4,128)} %param.20) | copy-start | bytes 388
  21.7 45.9 %collective-permute-start = (f32[40,128]{1,0:T(8,128)S(1)}, f32[40,128]{1,0:T(8,128)S(1)}, u32[]{:S(2)}, u32[]{:S(2)}) collective-permute-start(f32[40,128]{1,0:T(8,128)S(1)} %get-tuple-element.53), channel_id=1, source_target_pairs={{0,8},{8,16},{16,24},{24,32},{32,40},{40,48},{48,56},{56,64},{64,7... | collective-permute-start | bytes 61448 | tf_op jit(solution)/shard_map/ppermute | solution.py:544
  23.3 45.5 %collective-permute-start.1 = (f32[40,128]{1,0:T(8,128)S(1)}, f32[40,128]{1,0:T(8,128)S(1)}, u32[]{:S(2)}, u32[]{:S(2)}) collective-permute-start(f32[40,128]{1,0:T(8,128)S(1)} %get-tuple-element.54), channel_id=1, source_target_pairs={{0,120},{8,0},{16,8},{24,16},{32,24},{40,32},{48,40},{56,48},{64,5... | collective-permute-start | bytes 61448 | tf_op jit(solution)/shard_map/ppermute | solution.py:544
  27.3 41.5 %collective-permute-start.2 = (f32[40,128]{1,0:T(8,128)S(1)}, f32[40,128]{1,0:T(8,128)S(1)}, u32[]{:S(2)}, u32[]{:S(2)}) collective-permute-start(f32[40,128]{1,0:T(8,128)S(1)} %get-tuple-element.55), channel_id=1, source_target_pairs={{0,1},{1,2},{2,3},{3,4},{4,5},{5,6},{6,7},{7,0},{8,9},{9,10},{10,1... | collective-permute-start | bytes 61448 | tf_op jit(solution)/shard_map/ppermute | solution.py:544
  29.1 39.8 %collective-permute-start.3 = (f32[40,128]{1,0:T(8,128)S(1)}, f32[40,128]{1,0:T(8,128)S(1)}, u32[]{:S(2)}, u32[]{:S(2)}) collective-permute-start(f32[40,128]{1,0:T(8,128)S(1)} %get-tuple-element.56), channel_id=1, source_target_pairs={{0,7},{1,0},{2,1},{3,2},{4,3},{5,4},{6,5},{7,6},{8,15},{9,8},{10,9... | collective-permute-start | bytes 61448 | tf_op jit(solution)/shard_map/ppermute | solution.py:544
  29.7 59.1 %collective-permute-start.4 = (f32[64,128]{1,0:T(8,128)}, f32[64,128]{1,0:T(8,128)}, u32[]{:S(2)}, u32[]{:S(2)}) collective-permute-start(f32[64,128]{1,0:T(8,128)} %pad_bitcast_fusion.3.field.values.extra.last), channel_id=1, source_target_pairs={{0,1},{1,2},{2,3},{3,4},{4,5},{5,6},{6,7},{7,8},{8,9},{9,10},{10,1... | collective-permute-start | bytes 98312 | tf_op jit(solution)/shard_map/ppermute | solution.py:535
  32.6 61.5 %copy-start.28 = (s32[32]{0:T(128)}, s32[32]{0:T(128)S(1)}, u32[]{:S(2)}) copy-start(s32[32]{0:T(128)S(1)} %reshape.51.pattern) | copy-start | bytes 388
  39.0 39.2 %copy-start.51 = (f32[8,128]{1,0:T(8,128)S(1)}, f32[8,128]{1,0:T(8,128)}, u32[]{:S(2)}) copy-start(f32[8,128]{1,0:T(8,128)} %param.21) | copy-start | bytes 12292
  39.0 39.3 %copy-start.50 = (f32[8,3,128]{2,0,1:T(8,128)S(1)}, f32[8,3,128]{2,0,1:T(8,128)}, u32[]{:S(2)}) copy-start(f32[8,3,128]{2,0,1:T(8,128)} %param.22) | copy-start | bytes 36868
  39.0 39.3 %copy-start.44 = (f32[8,8,3,128]{3,1,2,0:T(8,128)S(1)}, f32[8,8,3,128]{3,1,2,0:T(8,128)}, u32[]{:S(2)}) copy-start(f32[8,8,3,128]{3,1,2,0:T(8,128)} %param.24) | copy-start | bytes 294916
  67.6 21.1 %collective-permute-start.5 = (f32[64,128]{1,0:T(8,128)}, f32[64,128]{1,0:T(8,128)}, u32[]{:S(2)}, u32[]{:S(2)}) collective-permute-start(f32[64,128]{1,0:T(8,128)} %shard_map.155), channel_id=1, source_target_pairs={{1,0},{2,1},{3,2},{4,3},{5,4},{6,5},{7,6},{8,7},{9,8},{10,9},{11,1... | collective-permute-start | bytes 98312 | tf_op jit(solution)/shard_map/ppermute | solution.py:539
  68.8 18.5 %all-to-all-start.1 = ((f32[128,2,128]{2,1,0:T(2,128)}), f32[128,2,128]{2,1,0:T(2,128)S(1)}, u32[]{:S(2)}, u32[]{:S(2)}) async-start(f32[128,2,128]{2,1,0:T(2,128)} %bitcast.53), calls=%async_computation.1 | async-start | bytes 262144 | tf_op jit(solution)/shard_map/all_to_all | solution.py:531
  78.2 15.9 %copy-start.8 = (f32[5,128,128]{2,1,0:T(8,128)}, f32[5,128,128]{2,1,0:T(8,128)S(1)}, u32[]{:S(2)}) copy-start(f32[5,128,128]{2,1,0:T(8,128)S(1)} %slice_bitcast_fusion.bottom) | copy-start | bytes 983044
  78.3 25.3 %copy-start.46 = (f32[8,3,128]{2,1,0:T(4,128)}, f32[8,3,128]{2,1,0:T(4,128)S(1)}, u32[]{:S(2)}) copy-start(f32[8,3,128]{2,1,0:T(4,128)S(1)} %copy.69) | copy-start | bytes 36868
  88.8 15.4 %all-to-all-start.2 = ((f32[128,2,128]{2,1,0:T(2,128)}), f32[128,2,128]{2,1,0:T(2,128)}, u32[]{:S(2)}, u32[]{:S(2)}) async-start(f32[128,2,128]{2,1,0:T(2,128)} %bitcast.7), calls=%async_computation.2 | async-start | bytes 262144 | tf_op jit(solution)/shard_map/all_to_all | solution.py:531
  104.2 20.6 %copy-start.43 = (f32[8,8,3,128]{3,2,1,0:T(4,128)S(1)}, f32[8,8,3,128]{3,2,1,0:T(4,128)}, u32[]{:S(2)}) copy-start(f32[8,8,3,128]{3,2,1,0:T(4,128)} %copy.70) | copy-start | bytes 294916
  104.2 24.2 %copy-start.1 = (f32[8,4,128,128]{3,2,1,0:T(8,128)S(1)}, f32[8,4,128,128]{3,2,1,0:T(8,128)}, u32[]{:S(2)}) copy-start(f32[8,4,128,128]{3,2,1,0:T(8,128)} %couplings.19) | copy-start | bytes 6291460
  104.2 24.2 %copy-start.29 = (s32[32]{0:T(128)S(1)}, s32[32]{0:T(128)}, u32[]{:S(2)}) copy-start(s32[32]{0:T(128)} %copy-done.28) | copy-start | bytes 388
  123.1 9.4 %copy-start.45 = (f32[8,8,3,128]{3,1,2,0:T(8,128)S(1)}, f32[8,8,3,128]{3,1,2,0:T(8,128)}, u32[]{:S(2)}) copy-start(f32[8,8,3,128]{3,1,2,0:T(8,128)} %param.24) | copy-start | bytes 294916
  123.1 3.1 %collective-permute-start.6 = (f32[64,128]{1,0:T(8,128)}, f32[64,128]{1,0:T(8,128)S(1)}, u32[]{:S(2)}, u32[]{:S(2)}) collective-permute-start(f32[64,128]{1,0:T(8,128)} %get-tuple-element.74.values.start), channel_id=1, source_target_pairs={{0,1},{1,2},{2,3},{3,4},{4,5},{5,6},{6,7},{7,8},{8,9},{9,10},{10,1... | collective-permute-start | bytes 98312 | tf_op jit(solution)/shard_map/ppermute | solution.py:535
  124.8 3.6 %collective-permute-start.7 = (f32[64,128]{1,0:T(8,128)}, f32[64,128]{1,0:T(8,128)S(1)}, u32[]{:S(2)}, u32[]{:S(2)}) collective-permute-start(f32[64,128]{1,0:T(8,128)} %get-tuple-element.75), channel_id=1, source_target_pairs={{1,0},{2,1},{3,2},{4,3},{5,4},{6,5},{7,6},{8,7},{9,8},{10,9},{11,1... | collective-permute-start | bytes 98312 | tf_op jit(solution)/shard_map/ppermute | solution.py:539
  132.3 6.1 %collective-permute-start.8 = (f32[64,128]{1,0:T(8,128)}, f32[64,128]{1,0:T(8,128)}, u32[]{:S(2)}, u32[]{:S(2)}) collective-permute-start(f32[64,128]{1,0:T(8,128)} %shard_map.158.image), channel_id=1, source_target_pairs={{0,1},{1,2},{2,3},{3,4},{4,5},{5,6},{6,7},{7,8},{8,9},{9,10},{10,1... | collective-permute-start | bytes 98312 | tf_op jit(solution)/shard_map/ppermute | solution.py:535
  143.8 21.7 %all-to-all-start.3 = ((f32[128,1,128]{2,1,0:T(1,128)}), f32[128,1,128]{2,1,0:T(1,128)}, u32[]{:S(2)}, u32[]{:S(2)}) async-start(f32[128,1,128]{2,1,0:T(1,128)} %bitcast.49), calls=%async_computation.3 | async-start | bytes 131072 | tf_op jit(solution)/shard_map/all_to_all | solution.py:531
  170.8 21.5 %copy-start.17 = (f32[64,128]{1,0:T(8,128)S(1)}, f32[64,128]{1,0:T(8,128)}, u32[]{:S(2)}) copy-start(f32[64,128]{1,0:T(8,128)} %copy-done.16) | copy-start | bytes 98308
  183.9 18.2 %all-to-all-start.4 = ((f32[128,2,128]{2,1,0:T(2,128)}), f32[128,2,128]{2,1,0:T(2,128)}, u32[]{:S(2)}, u32[]{:S(2)}) async-start(f32[128,2,128]{2,1,0:T(2,128)} %bitcast.52), calls=%async_computation.4 | async-start | bytes 262144 | tf_op jit(solution)/shard_map/all_to_all | solution.py:531
  195.7 12.0 %collective-permute-start.10 = (f32[64,128]{1,0:T(8,128)}, f32[64,128]{1,0:T(8,128)}, u32[]{:S(2)}, u32[]{:S(2)}) collective-permute-start(f32[64,128]{1,0:T(8,128)} %shard_map.165), channel_id=1, source_target_pairs={{1,0},{2,1},{3,2},{4,3},{5,4},{6,5},{7,6},{8,7},{9,8},{10,9},{11,1... | collective-permute-start | bytes 98312 | tf_op jit(solution)/shard_map/ppermute | solution.py:539
  196.8 10.9 %collective-permute-start.9 = (f32[64,128]{1,0:T(8,128)S(1)}, f32[64,128]{1,0:T(8,128)}, u32[]{:S(2)}, u32[]{:S(2)}) collective-permute-start(f32[64,128]{1,0:T(8,128)S(1)} %copy-done.17), channel_id=1, source_target_pairs={{0,1},{1,2},{2,3},{3,4},{4,5},{5,6},{6,7},{7,8},{8,9},{9,10},{10,1... | collective-permute-start | bytes 98312 | tf_op jit(solution)/shard_map/ppermute | solution.py:535
  207.7 19.7 %all-to-all-start.5 = ((f32[128,2,128]{2,1,0:T(2,128)}), f32[128,2,128]{2,1,0:T(2,128)S(1)}, u32[]{:S(2)}, u32[]{:S(2)}) async-start(f32[128,2,128]{2,1,0:T(2,128)} %bitcast.50), calls=%async_computation.5 | async-start | bytes 262144 | tf_op jit(solution)/shard_map/all_to_all | solution.py:531
  228.1 23.2 %copy-start.2 = (f32[8,4,128,128]{3,2,1,0:T(8,128)S(1)}, f32[8,4,128,128]{3,2,1,0:T(8,128)}, u32[]{:S(2)}) copy-start(f32[8,4,128,128]{3,2,1,0:T(8,128)} %couplings.19) | copy-start | bytes 6291460
  228.1 23.2 %copy-start.33 = (s32[32]{0:T(128)S(1)}, s32[32]{0:T(128)}, u32[]{:S(2)}) copy-start(s32[32]{0:T(128)} %copy-done.28) | copy-start | bytes 388
  228.1 32.8 %copy-start.13 = (f32[8,64,128]{2,1,0:T(8,128)S(1)}, f32[8,64,128]{2,1,0:T(8,128)}, u32[]{:S(2)}) copy-start(f32[8,64,128]{2,1,0:T(8,128)} %pad_bitcast_fusion.1.tested) | copy-start | bytes 786436
  228.1 32.8 %copy-start.35 = (f32[64,128]{1,0:T(8,128)S(1)}, f32[64,128]{1,0:T(8,128)}, u32[]{:S(2)}) copy-start(f32[64,128]{1,0:T(8,128)} %copy-done.34) | copy-start | bytes 98308
  247.0 28.8 %copy-start.11 = (f32[5,2,128,128]{3,2,1,0:T(8,128)S(1)}, f32[5,2,128,128]{3,2,1,0:T(8,128)}, u32[]{:S(2)}) copy-start(f32[5,2,128,128]{3,2,1,0:T(8,128)} %copy-done.10) | copy-start | bytes 1966084
  247.0 28.8 %copy-start.20 = (f32[5,128,128]{2,1,0:T(8,128)S(1)}, f32[5,128,128]{2,1,0:T(8,128)}, u32[]{:S(2)}) copy-start(f32[5,128,128]{2,1,0:T(8,128)} %copy-done.19) | copy-start | bytes 983044
  247.0 2.1 collective-permute-start.11
  247.8 3.6 %collective-permute-start.12 = (f32[64,128]{1,0:T(8,128)}, f32[64,128]{1,0:T(8,128)S(1)}, u32[]{:S(2)}, u32[]{:S(2)}) collective-permute-start(f32[64,128]{1,0:T(8,128)} %get-tuple-element.95), channel_id=1, source_target_pairs={{1,0},{2,1},{3,2},{4,3},{5,4},{6,5},{7,6},{8,7},{9,8},{10,9},{11,1... | collective-permute-start | bytes 98312 | tf_op jit(solution)/shard_map/ppermute | solution.py:539
  254.7 6.1 %collective-permute-start.13 = (f32[64,128]{1,0:T(8,128)S(1)}, f32[64,128]{1,0:T(8,128)S(1)}, u32[]{:S(2)}, u32[]{:S(2)}) collective-permute-start(f32[64,128]{1,0:T(8,128)S(1)} %shard_map.168.image), channel_id=1, source_target_pairs={{0,1},{1,2},{2,3},{3,4},{4,5},{5,6},{6,7},{7,8},{8,9},{9,10},{10,1... | collective-permute-start | bytes 98312 | tf_op jit(solution)/shard_map/ppermute | solution.py:535
  264.3 21.1 %all-to-all-start.6 = ((f32[128,1,128]{2,1,0:T(1,128)}), f32[128,1,128]{2,1,0:T(1,128)S(1)}, u32[]{:S(2)}, u32[]{:S(2)}) async-start(f32[128,1,128]{2,1,0:T(1,128)} %bitcast.25), calls=%async_computation.6 | async-start | bytes 131072 | tf_op jit(solution)/shard_map/all_to_all | solution.py:531
  275.8 9.6 %copy-start.15 = (f32[8,64,128]{2,1,0:T(8,128)S(1)}, f32[8,64,128]{2,1,0:T(8,128)}, u32[]{:S(2)}) copy-start(f32[8,64,128]{2,1,0:T(8,128)} %pad_bitcast_fusion.responses) | copy-start | bytes 786436
  275.8 9.6 %copy-start.22 = (f32[64,128]{1,0:T(8,128)S(1)}, f32[64,128]{1,0:T(8,128)}, u32[]{:S(2)}) copy-start(f32[64,128]{1,0:T(8,128)} %get-tuple-element.94.values.start) | copy-start | bytes 98308
  275.8 9.6 %copy-start.37 = (f32[64,128]{1,0:T(8,128)S(1)}, f32[64,128]{1,0:T(8,128)}, u32[]{:S(2)}) copy-start(f32[64,128]{1,0:T(8,128)} %copy-done.36) | copy-start | bytes 98308
  275.8 9.6 %copy-start.41 = (f32[16,128]{1,0:T(8,128)S(1)}, f32[16,128]{1,0:T(8,128)}, u32[]{:S(2)}) copy-start(f32[16,128]{1,0:T(8,128)} %copy-done.40) | copy-start | bytes 24580
  (26 other events, 31.0 us)
where the time goes:
time: 289 us; the launch traced here: 288 us
  Pallas kernels  126 us (44%)
  starting transfers between devices  82.4 us (29%)
  local copies, waits for them, and re-layouts  37.6 us (13%)
  waiting for transfers between devices  35.6 us (12%)
  other arithmetic  4.14 us (1%)
    pallas_call x4, Pallas kernels, whole(): pl.pallas_call(kernel, out_shape=outs, in_specs=[pl.BlockSpec(memory_spac...  79.5 us
    all_to_all x7, starting transfers between devices, exchange(): return lax.all_to_all(values, AXES, split_axis=0, concat_axis=0, tiled=True)  67.7 us
    pallas_call x19, Pallas kernels, run(): pl.pallas_call(kernel, out_shape=outs, in_specs=specs + [pl.BlockSpec()]...  46.4 us
    unnamed x118, local copies, waits for them, and re-layouts  30.6 us
    all_to_all x7, waiting for transfers between devices, exchange(): return lax.all_to_all(values, AXES, split_axis=0, concat_axis=0, tiled=True)  21.9 us
    ppermute x6, waiting for transfers between devices, forward(): lax.ppermute(values, AXES, [(i, (i + 1) % DEVICES) for i in range(DEVICES)])  9.27 us
    ppermute x4, starting transfers between devices, shift(): lax.ppermute(values, axis, [(i, (i + step) % count) for i in range(count)])  7.33 us
  transfers between devices with their start and end apart: 21, of which 12 were waited for; matrix products, arithmetic and copies ran while one was open for 5% of the time, Pallas kernels for 20%

commit v1 on v0

--- a/solution.py
+++ b/solution.py
@@ -143,17 +143,16 @@
 
 
 def pack_kernel(own, points, normals, support, geo, slot_row, slot_col):
-    across = jnp.broadcast_to(own[...].astype(F32), (128, 128))
-    along = across.T
+    along = jnp.broadcast_to(own[...].astype(F32), (128, 128))
+    across = along.T
     same = across == along
     row_rank = jnp.sum(jnp.where(same & (iota((128, 128), 0) < iota((128, 128), 1)), 1.0, 0.0), axis=0, keepdims=True)
     col_rank = jnp.sum(jnp.where(same & (iota((128, 128), 1) < iota((128, 128), 0)), 1.0, 0.0), axis=1, keepdims=True)
     slots = 2.0 * along[:1] + row_rank
     slot_row[...] = jnp.broadcast_to(slots, (8, 128))
     slot_col[...] = 2.0 * across + col_rank
-    ids = jnp.concatenate([support[...].astype(F32), jnp.zeros((128, 126), F32)], axis=1)
-    values = [points[:, axis, :] for axis in range(3)]
-    values += [normals[:, axis, :] for axis in range(3)]
+    ids = jnp.concatenate([support[...].astype(F32), jnp.zeros((126, 128), F32)], axis=0).T
+    values = [points[axis] for axis in range(3)] + [normals[axis] for axis in range(3)]
     values = jnp.concatenate(values + [ids], axis=1)
     high = values.astype(BF16)
     rest = values - high.astype(F32)
@@ -176,7 +175,7 @@
     row = iota((8, 128), 0)
     zero = jnp.zeros((8, 128), F32)
     for block in range(8):
-        tile = points[block] - 0.5
+        tile = points[:, block, :] - 0.5
         size = jnp.broadcast_to(jnp.sum(tile * tile, axis=0, keepdims=True), (8, 128))
         size_high = size.astype(BF16).astype(F32)
         size_mid = (size - size_high).astype(BF16).astype(F32)
@@ -246,17 +245,14 @@
             ).astype(BF16)
             for rank in range(2):
                 slot = (step * PEERS + peer) * 2 + rank
-                tiles, blocks = [], []
-                for k in range(2):
-                    block = support[slot * 2 + k]
-                    squared = jnp.maximum(dot_nn(table[rank * 8 + block], right), 1e-30)
-                    ratio = squared * lax.rsqrt(squared)
-                    reach = jnp.maximum(1.0 - ratio, 0.0)
-                    reach = reach * reach
-                    value = reach * reach * (4.0 * ratio + 1.0)
-                    tiles.append(jnp.concatenate(halves(value), axis=1))
-                    blocks.append(block)
-                tile = jnp.concatenate(tiles, axis=0)
+                blocks = [support[slot * 2 + k] for k in range(2)]
+                left = jnp.concatenate([table[rank * 8 + block] for block in blocks], axis=0)
+                squared = jnp.maximum(dot_nn(left, right), 1e-30)
+                ratio = squared * lax.rsqrt(squared)
+                reach = jnp.maximum(1.0 - ratio, 0.0)
+                reach = reach * reach
+                value = reach * reach * (4.0 * ratio + 1.0)
+                tile = jnp.concatenate(halves(value), axis=1)
                 phi[slot] = tile
                 rows.append(moved_row(wide, tile, blocks, normals[3 * rank : 3 * rank + 3]))
         motion[pl.ds(pl.multiple_of(step * 2 * PEERS, 8), 8), :] = jnp.concatenate(rows, axis=0)
@@ -272,24 +268,46 @@
     lax.fori_loop(0, STEPS, finish, 0)
 
 
-def motion_kernel(support, geo, field, phi_hbm, motion, wide, phi, sems):
-    fetch_tiles(phi_hbm, phi, sems)
-    spread_field(field, wide)
+def basis_kernel(first, support, geo, field, start, image, responses, phi_hbm, motion, wide, phi, sems):
+    def copy(step):
+        there = pl.ds(pl.multiple_of((first + step) * 2 * PEERS, 2 * PEERS), 2 * PEERS)
+        here = pl.ds(pl.multiple_of(step * 2 * PEERS, 2 * PEERS), 2 * PEERS)
+        return pltpu.make_async_copy(phi_hbm.at[there], phi.at[here], sems.at[step])
+
+    def begin(step, carry):
+        copy(step).start()
+        return carry
+
+    lax.fori_loop(0, STEPS // 2, begin, 0)
+    for block in range(8):
+        pieces = []
+        for axis in range(3):
+            line = pl.ds(block * 8 + axis, 1)
+            rows = [field[line, :], start[line, :], image[line, :]]
+            rows += [responses[h, line, :] for h in range(8)]
+            pieces.append(jnp.concatenate(rows + [jnp.zeros((5, 128), F32)], axis=0))
+        wide[block] = stacked_halves(jnp.concatenate(pieces, axis=0))
 
     def body(step, carry):
-        tile_copy(phi_hbm, phi, sems, step).wait()
-        rows = []
+        copy(step).wait()
         for index in range(2 * PEERS):
-            slot = step * PEERS * 2 + index
+            here = step * PEERS * 2 + index
+            slot = first * PEERS * 2 + here
             rank = index % 2
-            start = pl.multiple_of((step * PEERS + index // 2) * 16, 16)
-            normals = geo[pl.ds(start + 8, 8), :]
-            blocks = [support[slot * 2 + k] for k in range(2)]
-            rows.append(moved_row(wide, phi[slot], blocks, normals[3 * rank : 3 * rank + 3]))
-        motion[pl.ds(pl.multiple_of(step * 2 * PEERS, 8), 8), :] = jnp.concatenate(rows, axis=0)
+            place = pl.multiple_of(((first + step) * PEERS + index // 2) * 16, 16)
+            normals = geo[pl.ds(place + 8, 8), :]
+            left = jnp.concatenate([wide[support[slot * 2 + k]] for k in range(2)], axis=1)
+            moved = dot_nn(left, phi[here])
+            moved = moved[:, :128] + moved[:, 128:]
+            moved = moved[:48] + moved[48:]
+            total = moved[:16] * normals[3 * rank : 3 * rank + 1]
+            for axis in range(1, 3):
+                line = 3 * rank + axis
+                total = total + moved[16 * axis : 16 * axis + 16] * normals[line : line + 1]
+            motion[here] = total
         return carry
 
-    lax.fori_loop(0, STEPS, body, 0)
+    lax.fori_loop(0, STEPS // 2, body, 0)
 
 
 def wall_kernel(received, slot_row, slot_col, bottom, base, fresh, sent):
@@ -364,10 +382,11 @@
 
 
 def loads_kernel(
-    support, pattern, amounts, geo, phi_hbm, base, couplings, start, back, loads, phi, sems
+    support, pattern, amounts, geo, phi_hbm, base, couplings, start, back, l0, l1, l2, l3, phi, sems
 ):
     fetch_tiles(phi_hbm, phi, sems)
-    loads[...] = jnp.zeros((8, 8, 128), F32)
+    for loads in (l0, l1, l2, l3):
+        loads[...] = jnp.zeros((8, 8, 128), F32)
     row = iota((8, 128), 0)
 
     def body(step, carry):
@@ -386,12 +405,13 @@
                 term = term[:8] + term[8:]
                 for k in range(2):
                     block = support[slot * 2 + k]
+                    loads = ((l0, l1), (l2, l3))[rank][k]
                     loads[block] = loads[block] + term[:, k * 128 : k * 128 + 128]
         return carry
 
     lax.fori_loop(0, STEPS, body, 0)
     for block in range(8):
-        tile = loads[block]
+        tile = (l0[block] + l1[block]) + (l2[block] + l3[block])
         start[pl.ds(block * 8, 8), :] = base[pl.ds(block * 8, 8), :] + jnp.where(
             row < 3, tile + pltpu.roll(tile, 5, 0), 0.0
         )
@@ -430,8 +450,12 @@
 
 
 def solve_kernel(
-    count, received, memory, field, start, image, last, responses, estimate, residual, *more
+    count, received, memory, field, start, image, last, responses, *more
 ):
+    if count == 0:
+        halves_of, (estimate, residual, kept, saved, motion) = more[:2], more[2:]
+    else:
+        estimate, residual = more
     totals = row_sum(received[...])
 
     def lane(index):
@@ -491,7 +515,16 @@
         used = responses[h] if count == 0 or h > 0 else response - last[...]
         result = result - weight * used
     if count == 0:
-        kept, saved = more
+        one = jnp.ones((1, 1), F32)
+        mixture = jnp.concatenate(
+            [one, c0, c1, -system[:, 8:9], jnp.zeros((5, 1), F32)], axis=0
+        )
+        mixture = jnp.broadcast_to(mixture, (16, 128))
+        for half in range(2):
+            for chunk in range(16):
+                tiles = halves_of[half][chunk * 8 : chunk * 8 + 8]
+                place = half * 128 + chunk * 8
+                motion[place : place + 8, :] = jnp.sum(tiles * mixture[None], axis=1)
         estimate[...] = result
         residual[...] = change
         kept[...] = response
@@ -501,15 +534,17 @@
         )
     else:
         for block in range(8):
-            estimate[block] = result[block * 8 : block * 8 + 3]
-            residual[block] = change[block * 8 : block * 8 + 3]
+            for axis in range(3):
+                line = block * 8 + axis
+                estimate[axis, block : block + 1, :] = result[line : line + 1]
+                residual[axis, block : block + 1, :] = change[line : line + 1]
 
 
 def shape(*dims, dtype=F32):
     return jax.ShapeDtypeStruct(dims, dtype)
 
 
-def call(kernel, outs, scratch=(), scalars=0, cost=None, **kw):
+def call(kernel, outs, scratch=(), scalars=0, cost=None, room=14, **kw):
     specs = [pl.BlockSpec(memory_space=SMEM)] * scalars
 
     def run(*args):
@@ -519,7 +554,7 @@
             in_specs=specs + [pl.BlockSpec()] * (len(args) - scalars),
             out_specs=jax.tree.map(lambda _: pl.BlockSpec(), outs),
             scratch_shapes=list(scratch),
-            compiler_params=pltpu.CompilerParams(vmem_limit_bytes=14 << 20),
+            compiler_params=pltpu.CompilerParams(vmem_limit_bytes=room << 20),
             cost_estimate=cost,
             **kw,
         )(*args)
@@ -575,15 +610,19 @@
     )
 
 
-def find_motion(support, geo, field, phi):
+def basis_motion(half, support, geo, field, start, image, responses, phi):
     return whole(
-        motion_kernel,
+        functools.partial(basis_kernel, half * STEPS // 2),
         1,
-        [pl.BlockSpec()] * 2 + [RESIDENT],
+        [pl.BlockSpec()] * 5 + [RESIDENT],
         pl.BlockSpec(),
-        shape(256, 128),
-        [WIDE] + HELD,
-        (support, geo, field, phi),
+        shape(128, 16, 128),
+        [
+            pltpu.VMEM((8, 96, 128), BF16),
+            pltpu.VMEM((128, 256, 256), BF16),
+            pltpu.SemaphoreType.DMA((STEPS // 2,)),
+        ],
+        (support, geo, field, start, image, responses, phi),
     )
 
 
@@ -594,7 +633,7 @@
         [pl.BlockSpec()] * 2 + [RESIDENT] + [pl.BlockSpec()] * 2,
         [pl.BlockSpec(), pl.BlockSpec()],
         [shape(64, 128), shape(64, 128)],
-        [pltpu.VMEM((8, 8, 128), F32)] + HELD,
+        [pltpu.VMEM((8, 8, 128), F32)] * 4 + HELD,
         (support, pattern, amounts, geo, phi, base, couplings),
     )
 
@@ -622,8 +661,13 @@
 ):
     pattern = coupling_pattern.reshape(32)
     geo, slot_row, slot_col = call(
-        pack_kernel, [shape(2048, 128), shape(8, 128), shape(128, 128)]
-    )(owner_ids, surface_points, surface_normals, support_ids)
+        pack_kernel, [shape(2048, 128), shape(8, 128), shape(128, 128)], room=56
+    )(
+        owner_ids.T,
+        jnp.transpose(surface_points, (1, 0, 2)),
+        jnp.transpose(surface_normals, (1, 0, 2)),
+        support_ids.T,
+    )
     geo = exchange(geo)
     support = geo.reshape(128, 16, 128)[:, 6:8, :2].astype(jnp.int32).reshape(512)
     low_x, high_x, low_y, high_y = call(edges_kernel, [shape(40, 128)] * 4)(fluid_state)
@@ -644,7 +688,9 @@
         ),
         ((0, 0), (64, 0)),
     )
-    table = call(table_kernel, shape(16, 128, 64, dtype=BF16))(struct_points)
+    table = call(table_kernel, shape(16, 128, 64, dtype=BF16))(
+        jnp.transpose(struct_points, (1, 0, 2))
+    )
 
     def back_of(values):
         return call(back_kernel, shape(64, 128), scalars=1)(pattern, values, couplings)
@@ -652,7 +698,7 @@
     def applied(values, back, shift, gate=None):
         before, behind = forward(values), backward(back)
         if gate is not None:
-            before, behind, _ = lax.optimization_barrier((before, behind, gate))
+            values = lax.optimization_barrier((values, gate))[0]
         return call(
             functools.partial(apply_kernel, shift),
             shape(64, 128),
@@ -685,18 +731,25 @@
     memory = diagonal
     last = field
     for count in range(2):
-        if count > 0:
-            motion = find_motion(support, geo, field, phi)
         received = exchange(motion)
         fresh, sent = call(wall_kernel, [shape(5, 128, 128), shape(256, 128)])(
             received, slot_row, slot_col, bottom, base_bottom
         )
         amounts = exchange(sent)
-        base = load - applied(field, back_of(field), 0.0, sent)
-        fluid_parts.append(fluid((1, 2, 3) if count == 0 else (6, 7), sent))
+        ready = lax.optimization_barrier((field, motion))[0]
+        stiff = applied(ready, back_of(ready), 0.0, sent)
+        base = load - stiff
+        fluid_parts.append(fluid((1, 2, 3) if count == 0 else (4,), sent))
         amounts, fluid_parts[-1] = lax.optimization_barrier((amounts, fluid_parts[-1]))
         start, back = find_loads(support, pattern, amounts, geo, phi, base, couplings)
         image = applied(start, back, SHIFT)
+        ahead = forward(image)
+        if count == 0:
+            first_half = basis_motion(0, support, geo, field, start, image, responses, phi)
+            ahead, first_half = lax.optimization_barrier((ahead, first_half))
+        else:
+            fluid_parts.append(fluid((5, 6, 7), image))
+            ahead, fluid_parts[-1] = lax.optimization_barrier((ahead, fluid_parts[-1]))
         row = call(
             sums_kernel,
             shape(128, 128),
@@ -706,7 +759,7 @@
             pattern,
             start,
             image,
-            forward(image),
+            ahead,
             diagonal,
             couplings,
             tested,
@@ -715,21 +768,36 @@
         )
         totals = exchange(row)
         if count == 0:
-            fluid_parts.append(fluid((4, 5), row))
-            totals, fluid_parts[-1] = lax.optimization_barrier((totals, fluid_parts[-1]))
+            gated = lax.optimization_barrier((start, image, row))
+            final_half = basis_motion(
+                1, support, geo, field, gated[0], gated[1], responses, phi
+            )
+            totals, final_half = lax.optimization_barrier((totals, final_half))
         solve = functools.partial(solve_kernel, count)
         if count == 0:
-            outs = [shape(64, 128), shape(64, 128), shape(64, 128), shape(16, 128)]
-            field, extra, last, memory = call(solve, outs)(
-                totals, jnp.zeros((16, 128), F32), field, start, image, last, responses
+            outs = [shape(64, 128)] * 3 + [shape(16, 128), shape(256, 128)]
+            field, extra, last, memory, motion = call(solve, outs, room=56)(
+                totals,
+                jnp.zeros((16, 128), F32),
+                field,
+                start,
+                image,
+                last,
+                responses,
+                first_half,
+                final_half,
             )
         else:
-            outs = [shape(8, 3, 128), shape(8, 3, 128)]
+            outs = [shape(3, 8, 128), shape(3, 8, 128)]
             estimate, residual = call(solve, outs)(
                 totals, memory, field, start, image, last, responses
             )
     new_state = jnp.concatenate([fresh[:, None]] + fluid_parts, axis=1)
-    return (new_state, estimate, residual)
+    return (
+        new_state,
+        jnp.transpose(estimate, (1, 0, 2)),
+        jnp.transpose(residual, (1, 0, 2)),
+    )
 
 
 def solution(mesh):

time: 289 us -> 275 us (0.952)
  local copies, waits for them, and re-layouts: 37.6 us -> 20.5 us
  Pallas kernels: 126 us -> 134 us
  waiting for transfers between devices: 35.6 us -> 29.9 us
  starting transfers between devices: 82.4 us -> 85.3 us
    unnamed x118 -> x117, local copies, waits for them, and re-layouts: 30.6 us -> 15.7 us
    ppermute x6, waiting for transfers between devices: 9.27 us -> 3.58 us  [forward(): lax.ppermute(values, AXES, [(i, (i + 1) % DEVICES) for i in range(DEVICES)])]
    pallas_call x19, Pallas kernels: 46.4 us -> 50.3 us  [run(): pl.pallas_call(kernel, out_shape=outs, in_specs=specs + [pl.BlockSpec()]...]
    pallas_call x4 -> x5, Pallas kernels: 79.5 us -> 83.3 us  [whole(): pl.pallas_call(kernel, out_shape=outs, in_specs=[pl.BlockSpec(memory_spac...]
    all_to_all x7, starting transfers between devices: 67.7 us -> 71.2 us  [exchange(): return lax.all_to_all(values, AXES, split_axis=0, concat_axis=0, tiled=True)]
  transfers between devices with their start and end apart: 21 -> 21, of which waited for: 12 -> 11; matrix products, arithmetic and copies ran while one was open for 5% -> 3% of each run, Pallas kernels for 20% -> 27%
where the time goes in v1:
time: 275 us; the launch traced here: 274 us
  Pallas kernels  134 us (49%)
  starting transfers between devices  85.3 us (31%)
  waiting for transfers between devices  29.9 us (11%)
  local copies, waits for them, and re-layouts  20.5 us (7%)
  other arithmetic  2.99 us (1%)
    pallas_call x5, Pallas kernels, whole(): pl.pallas_call(kernel, out_shape=outs, in_specs=[pl.BlockSpec(memory_spac...  83.3 us
    all_to_all x7, starting transfers between devices, exchange(): return lax.all_to_all(values, AXES, split_axis=0, concat_axis=0, tiled=True)  71.2 us
    pallas_call x19, Pallas kernels, run(): pl.pallas_call(kernel, out_shape=outs, in_specs=specs + [pl.BlockSpec()]...  50.3 us
    all_to_all x7, waiting for transfers between devices, exchange(): return lax.all_to_all(values, AXES, split_axis=0, concat_axis=0, tiled=True)  21.9 us
    unnamed x117, local copies, waits for them, and re-layouts  15.7 us
    ppermute x4, starting transfers between devices, shift(): lax.ppermute(values, axis, [(i, (i + step) % count) for i in range(count)])  7.33 us
    ppermute x6, starting transfers between devices, forward(): lax.ppermute(values, AXES, [(i, (i + 1) % DEVICES) for i in range(DEVICES)])  5.55 us
  transfers between devices with their start and end apart: 21, of which 11 were waited for; matrix products, arithmetic and copies ran while one was open for 3% of the time, Pallas kernels for 27%

profile of v1, /device:TPU:1, one launch (start us, length us, event | category | flops | bytes accessed | tf_op | source)
XLA Modules:
  0.0 273.9 jit_solution(6037607273201983258)
XLA Ops:
  0.7 2.8 %shard_map.148 = (f32[2048,128]{1,0:T(8,128)}, f32[8,128]{1,0:T(8,128)}, f32[128,128]{1,0:T(8,128)}) custom-call(s32[1,128]{1,0:T(1,128)} %bitcast.68, f32[3,128,128]{2,1,0:T(8,128)} %bitcast.63, f32[3,128,128]{2,1,0:T(8,128)} %bitcast.64, s32[2,128]{1,0:T(2,128)} %bitcast.67), custom_call_target="tpu_custom_call" | custom-call | tf_op jit(solution)/shard_map/pallas_call | solution.py:551
  3.4 11.5 %all-to-all-start = ((f32[128,16,128]{2,1,0:T(8,128)}), f32[128,16,128]{2,1,0:T(8,128)S(1)}, u32[]{:S(2)}, u32[]{:S(2)}) async-start(f32[128,16,128]{2,1,0:T(8,128)} %bitcast.61), calls=%async_computation | async-start | bytes 2097152 | tf_op jit(solution)/shard_map/all_to_all | solution.py:566
  15.0 1.7 copy-done.3
  16.7 1.7 shard_map.149
  18.4 1.6 collective-permute-start
  20.0 4.0 %collective-permute-start.1 = (f32[40,128]{1,0:T(8,128)S(1)}, f32[40,128]{1,0:T(8,128)S(1)}, u32[]{:S(2)}, u32[]{:S(2)}) collective-permute-start(f32[40,128]{1,0:T(8,128)S(1)} %get-tuple-element.61), channel_id=1, source_target_pairs={{0,120},{8,0},{16,8},{24,16},{32,24},{40,32},{48,40},{56,48},{64,5... | collective-permute-start | bytes 61448 | tf_op jit(solution)/shard_map/ppermute | solution.py:579
  24.0 1.8 collective-permute-start.2
  29.3 4.9 %all-to-all-done = f32[128,16,128]{2,1,0:T(8,128)S(1)} async-done(((f32[128,16,128]{2,1,0:T(8,128)}), f32[128,16,128]{2,1,0:T(8,128)S(1)}, u32[]{:S(2)}, u32[]{:S(2)}) %all-to-all-start) | async-done | bytes 1048608 | tf_op jit(solution)/shard_map/all_to_all | solution.py:566
  35.1 28.8 %shard_map.151 = (bf16[256,256,256]{2,1,0:T(8,128)(2,1)}, f32[256,128]{1,0:T(8,128)}) custom-call(s32[512]{0:T(512)} %reshape.51.support, f32[2048,128]{1,0:T(8,128)} %bitcast.56, bf16[16,128,64]{2,1,0:T(8,128)(2,1)} %copy-done.19, f32[64,128]{1,0:T(8,128)} %pad_bitcast_fusion.3.field.values.extra.last), custom_call_target="tpu_custom_call" | custom-call | flops 2000000000 | bytes 40000000 | tf_op jit(solution)/shard_map/pallas_call | solution.py:590
  64.0 4.6 %all-to-all-start.1 = ((f32[128,2,128]{2,1,0:T(2,128)}), f32[128,2,128]{2,1,0:T(2,128)S(1)}, u32[]{:S(2)}, u32[]{:S(2)}) async-start(f32[128,2,128]{2,1,0:T(2,128)} %bitcast.65), calls=%async_computation.1 | async-start | bytes 262144 | tf_op jit(solution)/shard_map/all_to_all | solution.py:566
  69.5 1.7 collective-permute-start.4
  71.2 2.7 shard_map.155
  74.5 1.7 copy-done.4
  76.3 1.5 shard_map.152
  79.3 1.5 shard_map.153
  80.7 10.3 %all-to-all-start.2 = ((f32[128,2,128]{2,1,0:T(2,128)}), f32[128,2,128]{2,1,0:T(2,128)}, u32[]{:S(2)}, u32[]{:S(2)}) async-start(f32[128,2,128]{2,1,0:T(2,128)} %bitcast.12), calls=%async_computation.2 | async-start | bytes 262144 | tf_op jit(solution)/shard_map/all_to_all | solution.py:566
  91.1 1.7 copy-done.5
  92.8 4.8 %shard_map.154 = f32[5,3,128,128]{3,2,1,0:T(8,128)S(1)} custom-call(f32[5,8,128,128]{3,2,1,0:T(8,128)S(1)} %copy-done.5, f32[40,128]{1,0:T(8,128)S(1)} %collective-permute-done.low_x, f32[40,128]{1,0:T(8,128)S(1)} %collective-permute-done.1.high_x, f32[40,128]{1,0:T(8,128)S(1)} %collective-permute-done.2.low_y, f32[40,128]{1,0:T(8,128)S(1)} %collective-permute-done.3.high_y), custom_call_target="tpu_custom_call" | custom-call | flops 120000000 | bytes 2100000 | tf_op jit(solution)/shard_map/pallas_call | solution.py:551
  97.7 2.8 %shard_map.156 = f32[64,128]{1,0:T(8,128)S(1)} custom-call(s32[32]{0:T(128)S(1)} %copy-done.36, f32[64,128]{1,0:T(8,128)S(1)} %copy-done.13, f32[64,128]{1,0:T(8,128)} %collective-permute-done.4.before, f32[64,128]{1,0:T(8,128)} %collective-permute-done.5.behind, f32[64,128]{1,0:T(8,128)S(1)} %pad_bitcast_fusion.4.diagonal, f32[8,4,128,128]{3,2,1,0:T(8,128)S(1)} %copy-done), custom_call_target="tpu_custom_call" | custom-call | tf_op jit(solution)/shard_map/pallas_call | solution.py:551
  101.2 18.4 %shard_map.157 = (f32[64,128]{1,0:T(8,128)}, f32[64,128]{1,0:T(8,128)}) custom-call(s32[512]{0:T(512)} %reshape.51.support, s32[32]{0:T(128)} %copy-done.35, f32[256,128]{1,0:T(8,128)} %bitcast.13.amounts, f32[2048,128]{1,0:T(8,128)} %bitcast.57, bf16[256,256,256]{2,1,0:T(8,128)(2,1)} %get-tuple-element.78.phi_hbm, f32[64,128]{1,0:T(8,128)} %fusion.2.base, ...), custom_call_target="tpu_custom_call" | custom-call | flops 2000000000 | bytes 40000000 | tf_op jit(solution)/shard_map/pallas_call | solution.py:590
  119.5 1.8 collective-permute-start.6
  122.6 2.2 collective-permute-done.7.behind
  125.6 2.6 shard_map.158.image
  128.8 8.7 %shard_map.159.more_0_ = f32[128,16,128]{2,1,0:T(8,128)} custom-call(s32[512]{0:T(512)} %reshape.51.support, f32[2048,128]{1,0:T(8,128)} %bitcast.58, f32[64,128]{1,0:T(8,128)} %pad_bitcast_fusion.3.field.values.extra.last, f32[64,128]{1,0:T(8,128)} %get-tuple-element.84.values.start, f32[64,128]{1,0:T(8,128)} %copy-done.17, ...), custom_call_target="tpu_custom_call" | custom-call | flops 2000000000 | bytes 40000000 | tf_op jit(solution)/shard_map/pallas_call | solution.py:590
  138.4 3.5 %shard_map.160 = f32[128,128]{1,0:T(8,128)} custom-call(s32[32]{0:T(128)S(1)} %copy-done.37, f32[64,128]{1,0:T(8,128)S(1)} %copy-done.16, f32[64,128]{1,0:T(8,128)S(1)} %copy-done.18, f32[64,128]{1,0:T(8,128)S(1)} %collective-permute-done.8.before, f32[64,128]{1,0:T(8,128)S(1)} %pad_bitcast_fusion.4.diagonal, f32[8,4,128,128]{3,2,1,0:T(8,128)S(1)} %copy-done.1, ...), custom_call_target="tpu_custom_call" | custom-call | tf_op jit(solution)/shard_map/pallas_call | solution.py:551
  141.9 13.2 %all-to-all-start.3 = ((f32[128,1,128]{2,1,0:T(1,128)}), f32[128,1,128]{2,1,0:T(1,128)S(1)}, u32[]{:S(2)}, u32[]{:S(2)}) async-start(f32[128,1,128]{2,1,0:T(1,128)} %bitcast.21), calls=%async_computation.3 | async-start | bytes 131072 | tf_op jit(solution)/shard_map/all_to_all | solution.py:566
  155.1 8.7 %shard_map.161.more_1_ = f32[128,16,128]{2,1,0:T(8,128)} custom-call(s32[512]{0:T(512)} %reshape.51.support, f32[2048,128]{1,0:T(8,128)} %bitcast.59, f32[64,128]{1,0:T(8,128)} %pad_bitcast_fusion.3.field.values.extra.last, f32[64,128]{1,0:T(8,128)} %get-tuple-element.84.values.start, f32[64,128]{1,0:T(8,128)} %copy-done.17, ...), custom_call_target="tpu_custom_call" | custom-call | flops 2000000000 | bytes 40000000 | tf_op jit(solution)/shard_map/pallas_call | solution.py:590
  165.8 3.9 %shard_map.162 = (f32[64,128]{1,0:T(8,128)}, f32[64,128]{1,0:T(8,128)}, f32[64,128]{1,0:T(8,128)}, f32[16,128]{1,0:T(8,128)}, f32[256,128]{1,0:T(8,128)}) custom-call(f32[128,128]{1,0:T(8,128)} %bitcast.62, f32[16,128]{1,0:T(8,128)} %broadcast_in_dim.16.memory, f32[64,128]{1,0:T(8,128)} %pad_bitcast_fusion.3.field.values.extra.last, ...), custom_call_target="tpu_custom_call" | custom-call | tf_op jit(solution)/shard_map/pallas_call | solution.py:551
  169.6 9.5 %all-to-all-start.4 = ((f32[128,2,128]{2,1,0:T(2,128)}), f32[128,2,128]{2,1,0:T(2,128)}, u32[]{:S(2)}, u32[]{:S(2)}) async-start(f32[128,2,128]{2,1,0:T(2,128)} %bitcast.66), calls=%async_computation.4 | async-start | bytes 262144 | tf_op jit(solution)/shard_map/all_to_all | solution.py:566
  179.2 2.9 %shard_map.165 = f32[64,128]{1,0:T(8,128)} custom-call(s32[32]{0:T(128)S(1)} %copy-done.37, f32[64,128]{1,0:T(8,128)} %get-tuple-element.101.values.field, f32[8,4,128,128]{3,2,1,0:T(8,128)S(1)} %copy-done.1), custom_call_target="tpu_custom_call" | custom-call | tf_op jit(solution)/shard_map/pallas_call | solution.py:551
  183.8 5.1 %all-to-all-done.4 = f32[128,2,128]{2,1,0:T(2,128)} async-done(((f32[128,2,128]{2,1,0:T(2,128)}), f32[128,2,128]{2,1,0:T(2,128)}, u32[]{:S(2)}, u32[]{:S(2)}) %all-to-all-start.4) | async-done | bytes 131104 | tf_op jit(solution)/shard_map/all_to_all | solution.py:566
  190.7 1.7 shard_map.163
  193.8 9.8 %all-to-all-start.5 = ((f32[128,2,128]{2,1,0:T(2,128)}), f32[128,2,128]{2,1,0:T(2,128)}, u32[]{:S(2)}, u32[]{:S(2)}) async-start(f32[128,2,128]{2,1,0:T(2,128)} %bitcast.54), calls=%async_computation.5 | async-start | bytes 262144 | tf_op jit(solution)/shard_map/all_to_all | solution.py:566
  203.7 1.7 copy-done.6
  205.4 1.6 shard_map.164
  207.1 2.9 %shard_map.166 = f32[64,128]{1,0:T(8,128)S(1)} custom-call(s32[32]{0:T(128)S(1)} %copy-done.37, f32[64,128]{1,0:T(8,128)} %get-tuple-element.101.values.field, f32[64,128]{1,0:T(8,128)} %collective-permute-done.9.before, f32[64,128]{1,0:T(8,128)} %collective-permute-done.10.behind, f32[64,128]{1,0:T(8,128)S(1)} %pad_bitcast_fusion.4.diagonal, ...), custom_call_target="tpu_custom_call" | custom-call | tf_op jit(solution)/shard_map/pallas_call | solution.py:551
  210.6 2.7 all-to-all-done.5
  213.3 18.7 %shard_map.167 = (f32[64,128]{1,0:T(8,128)}, f32[64,128]{1,0:T(8,128)}) custom-call(s32[512]{0:T(512)} %reshape.51.support, s32[32]{0:T(128)} %copy-done.35, f32[256,128]{1,0:T(8,128)} %bitcast.27.amounts, f32[2048,128]{1,0:T(8,128)} %bitcast.60, bf16[256,256,256]{2,1,0:T(8,128)(2,1)} %get-tuple-element.78.phi_hbm, f32[64,128]{1,0:T(8,128)} %fusion.1.base, ...), custom_call_target="tpu_custom_call" | custom-call | flops 2000000000 | bytes 40000000 | tf_op jit(solution)/shard_map/pallas_call | solution.py:590
  233.0 1.3 collective-permute-done.11.before
  234.3 2.2 collective-permute-done.12.behind
  237.2 2.6 shard_map.168.image
  240.0 4.7 %shard_map.169 = f32[5,3,128,128]{3,2,1,0:T(8,128)S(1)} custom-call(f32[5,8,128,128]{3,2,1,0:T(8,128)S(1)} %copy-done.7, f32[40,128]{1,0:T(8,128)S(1)} %copy-done.21, f32[40,128]{1,0:T(8,128)S(1)} %copy-done.23, f32[40,128]{1,0:T(8,128)S(1)} %copy-done.25, f32[40,128]{1,0:T(8,128)S(1)} %copy-done.27), custom_call_target="tpu_custom_call" | custom-call | flops 120000000 | bytes 2100000 | tf_op jit(solution)/shard_map/pallas_call | solution.py:551
  244.7 1.4 collective-permute-done.13.before
  246.1 3.5 %shard_map.170 = f32[128,128]{1,0:T(8,128)} custom-call(s32[32]{0:T(128)S(1)} %copy-done.38, f32[64,128]{1,0:T(8,128)S(1)} %copy-done.30, f32[64,128]{1,0:T(8,128)S(1)} %shard_map.168.image, f32[64,128]{1,0:T(8,128)S(1)} %collective-permute-done.13.before, f32[64,128]{1,0:T(8,128)S(1)} %pad_bitcast_fusion.4.diagonal, f32[8,4,128,128]{3,2,1,0:T(8,128)S(1)} %copy-done.2, ...), custom_call_target="tpu_custom_call" | custom-call | tf_op jit(solution)/shard_map/pallas_call | solution.py:551
  249.6 12.3 %all-to-all-start.6 = ((f32[128,1,128]{2,1,0:T(1,128)}), f32[128,1,128]{2,1,0:T(1,128)S(1)}, u32[]{:S(2)}, u32[]{:S(2)}) async-start(f32[128,1,128]{2,1,0:T(1,128)} %bitcast.29), calls=%async_computation.6 | async-start | bytes 131072 | tf_op jit(solution)/shard_map/all_to_all | solution.py:566
  262.0 1.7 pad_maximum_fusion
  263.7 7.7 %all-to-all-done.6 = f32[128,1,128]{2,1,0:T(1,128)S(1)} async-done(((f32[128,1,128]{2,1,0:T(1,128)}), f32[128,1,128]{2,1,0:T(1,128)S(1)}, u32[]{:S(2)}, u32[]{:S(2)}) %all-to-all-start.6) | async-done | bytes 65568 | tf_op jit(solution)/shard_map/all_to_all | solution.py:566
  271.4 2.5 shard_map.171
  (152 shorter events, 21.1 us)
Async XLA Ops:
  0.6 25.1 %copy-start.52 = (f32[8,3,128]{2,0,1:T(8,128)S(1)}, f32[8,3,128]{2,0,1:T(8,128)}, u32[]{:S(2)}) copy-start(f32[8,3,128]{2,0,1:T(8,128)} %param.23) | copy-start | bytes 36868
  0.6 25.1 %copy-start.43 = (f32[8,3,128]{2,0,1:T(8,128)S(1)}, f32[8,3,128]{2,0,1:T(8,128)}, u32[]{:S(2)}) copy-start(f32[8,3,128]{2,0,1:T(8,128)} %param.18) | copy-start | bytes 36868
  3.4 23.4 %copy-start.51 = (f32[8,8,3,128]{3,1,2,0:T(8,128)S(1)}, f32[8,8,3,128]{3,1,2,0:T(8,128)}, u32[]{:S(2)}) copy-start(f32[8,8,3,128]{3,1,2,0:T(8,128)} %param.25) | copy-start | bytes 294916
  3.4 23.4 %copy-start.46 = (f32[8,8,3,128]{3,1,2,0:T(8,128)S(1)}, f32[8,8,3,128]{3,1,2,0:T(8,128)}, u32[]{:S(2)}) copy-start(f32[8,8,3,128]{3,1,2,0:T(8,128)} %param.24) | copy-start | bytes 294916
  3.4 30.7 %all-to-all-start = ((f32[128,16,128]{2,1,0:T(8,128)}), f32[128,16,128]{2,1,0:T(8,128)S(1)}, u32[]{:S(2)}, u32[]{:S(2)}) async-start(f32[128,16,128]{2,1,0:T(8,128)} %bitcast.61), calls=%async_computation | async-start | bytes 2097152 | tf_op jit(solution)/shard_map/all_to_all | solution.py:566
  18.4 45.5 %collective-permute-start = (f32[40,128]{1,0:T(8,128)S(1)}, f32[40,128]{1,0:T(8,128)S(1)}, u32[]{:S(2)}, u32[]{:S(2)}) collective-permute-start(f32[40,128]{1,0:T(8,128)S(1)} %get-tuple-element.60), channel_id=1, source_target_pairs={{0,8},{8,16},{16,24},{24,32},{32,40},{40,48},{48,56},{56,64},{64,7... | collective-permute-start | bytes 61448 | tf_op jit(solution)/shard_map/ppermute | solution.py:579
  20.0 44.0 %collective-permute-start.1 = (f32[40,128]{1,0:T(8,128)S(1)}, f32[40,128]{1,0:T(8,128)S(1)}, u32[]{:S(2)}, u32[]{:S(2)}) collective-permute-start(f32[40,128]{1,0:T(8,128)S(1)} %get-tuple-element.61), channel_id=1, source_target_pairs={{0,120},{8,0},{16,8},{24,16},{32,24},{40,32},{48,40},{56,48},{64,5... | collective-permute-start | bytes 61448 | tf_op jit(solution)/shard_map/ppermute | solution.py:579
  24.0 40.0 %collective-permute-start.2 = (f32[40,128]{1,0:T(8,128)S(1)}, f32[40,128]{1,0:T(8,128)S(1)}, u32[]{:S(2)}, u32[]{:S(2)}) collective-permute-start(f32[40,128]{1,0:T(8,128)S(1)} %get-tuple-element.62), channel_id=1, source_target_pairs={{0,1},{1,2},{2,3},{3,4},{4,5},{5,6},{6,7},{7,0},{8,9},{9,10},{10,1... | collective-permute-start | bytes 61448 | tf_op jit(solution)/shard_map/ppermute | solution.py:579
  25.8 38.2 %collective-permute-start.3 = (f32[40,128]{1,0:T(8,128)S(1)}, f32[40,128]{1,0:T(8,128)S(1)}, u32[]{:S(2)}, u32[]{:S(2)}) collective-permute-start(f32[40,128]{1,0:T(8,128)S(1)} %get-tuple-element.63), channel_id=1, source_target_pairs={{0,7},{1,0},{2,1},{3,2},{4,3},{5,4},{6,5},{7,6},{8,15},{9,8},{10,9... | collective-permute-start | bytes 61448 | tf_op jit(solution)/shard_map/ppermute | solution.py:579
  29.3 49.3 %copy-start.9 = (f32[5,128,128]{2,1,0:T(8,128)}, f32[5,128,128]{2,1,0:T(8,128)S(1)}, u32[]{:S(2)}) copy-start(f32[5,128,128]{2,1,0:T(8,128)S(1)} %slice_bitcast_fusion.bottom) | copy-start | bytes 983044
  35.1 34.2 %copy-start.55 = (s32[8,4]{0,1:T(4,128)S(1)}, s32[8,4]{0,1:T(4,128)}, u32[]{:S(2)}) copy-start(s32[8,4]{0,1:T(4,128)} %param.20) | copy-start | bytes 388
  35.1 34.4 %copy-start.13 = (f32[64,128]{1,0:T(8,128)S(1)}, f32[64,128]{1,0:T(8,128)}, u32[]{:S(2)}) copy-start(f32[64,128]{1,0:T(8,128)} %pad_bitcast_fusion.3.field.values.extra.last) | copy-start | bytes 98308
  35.1 36.1 %copy-start = (f32[8,4,128,128]{3,2,1,0:T(8,128)S(1)}, f32[8,4,128,128]{3,2,1,0:T(8,128)}, u32[]{:S(2)}) copy-start(f32[8,4,128,128]{3,2,1,0:T(8,128)} %couplings.19) | copy-start | bytes 6291460
  63.9 10.0 %copy-start.54 = (f32[8,128]{1,0:T(8,128)S(1)}, f32[8,128]{1,0:T(8,128)}, u32[]{:S(2)}) copy-start(f32[8,128]{1,0:T(8,128)} %param.21) | copy-start | bytes 12292
  63.9 10.0 %copy-start.53 = (f32[8,3,128]{2,0,1:T(8,128)S(1)}, f32[8,3,128]{2,0,1:T(8,128)}, u32[]{:S(2)}) copy-start(f32[8,3,128]{2,0,1:T(8,128)} %param.22) | copy-start | bytes 36868
  63.9 27.1 %copy-start.20 = (f32[40,128]{1,0:T(8,128)}, f32[40,128]{1,0:T(8,128)S(1)}, u32[]{:S(2)}) copy-start(f32[40,128]{1,0:T(8,128)S(1)} %collective-permute-done.low_x) | copy-start | bytes 61444
  64.0 27.1 %copy-start.22 = (f32[40,128]{1,0:T(8,128)}, f32[40,128]{1,0:T(8,128)S(1)}, u32[]{:S(2)}) copy-start(f32[40,128]{1,0:T(8,128)S(1)} %collective-permute-done.1.high_x) | copy-start | bytes 61444
  64.0 27.1 %copy-start.24 = (f32[40,128]{1,0:T(8,128)}, f32[40,128]{1,0:T(8,128)S(1)}, u32[]{:S(2)}) copy-start(f32[40,128]{1,0:T(8,128)S(1)} %collective-permute-done.2.low_y) | copy-start | bytes 61444
  64.0 27.1 %copy-start.26 = (f32[40,128]{1,0:T(8,128)}, f32[40,128]{1,0:T(8,128)S(1)}, u32[]{:S(2)}) copy-start(f32[40,128]{1,0:T(8,128)S(1)} %collective-permute-done.3.high_y) | copy-start | bytes 61444
  64.0 14.6 %all-to-all-start.1 = ((f32[128,2,128]{2,1,0:T(2,128)}), f32[128,2,128]{2,1,0:T(2,128)S(1)}, u32[]{:S(2)}, u32[]{:S(2)}) async-start(f32[128,2,128]{2,1,0:T(2,128)} %bitcast.65), calls=%async_computation.1 | async-start | bytes 262144 | tf_op jit(solution)/shard_map/all_to_all | solution.py:566
  69.5 28.1 %collective-permute-start.4 = (f32[64,128]{1,0:T(8,128)S(1)}, f32[64,128]{1,0:T(8,128)}, u32[]{:S(2)}, u32[]{:S(2)}) collective-permute-start(f32[64,128]{1,0:T(8,128)S(1)} %copy-done.13), channel_id=1, source_target_pairs={{0,1},{1,2},{2,3},{3,4},{4,5},{5,6},{6,7},{7,8},{8,9},{9,10},{10,1... | collective-permute-start | bytes 98312 | tf_op jit(solution)/shard_map/ppermute | solution.py:570
  73.9 23.8 %collective-permute-start.5 = (f32[64,128]{1,0:T(8,128)}, f32[64,128]{1,0:T(8,128)}, u32[]{:S(2)}, u32[]{:S(2)}) collective-permute-start(f32[64,128]{1,0:T(8,128)} %shard_map.155), channel_id=1, source_target_pairs={{1,0},{2,1},{3,2},{4,3},{5,4},{6,5},{7,6},{8,7},{9,8},{10,9},{11,1... | collective-permute-start | bytes 98312 | tf_op jit(solution)/shard_map/ppermute | solution.py:574
  80.7 20.4 %all-to-all-start.2 = ((f32[128,2,128]{2,1,0:T(2,128)}), f32[128,2,128]{2,1,0:T(2,128)}, u32[]{:S(2)}, u32[]{:S(2)}) async-start(f32[128,2,128]{2,1,0:T(2,128)} %bitcast.12), calls=%async_computation.2 | async-start | bytes 262144 | tf_op jit(solution)/shard_map/all_to_all | solution.py:566
  101.2 20.1 %copy-start.47 = (f32[8,8,3,128]{3,1,2,0:T(8,128)S(1)}, f32[8,8,3,128]{3,1,2,0:T(8,128)}, u32[]{:S(2)}) copy-start(f32[8,8,3,128]{3,1,2,0:T(8,128)} %param.24) | copy-start | bytes 294916
  101.2 23.7 %copy-start.1 = (f32[8,4,128,128]{3,2,1,0:T(8,128)S(1)}, f32[8,4,128,128]{3,2,1,0:T(8,128)}, u32[]{:S(2)}) copy-start(f32[8,4,128,128]{3,2,1,0:T(8,128)} %couplings.19) | copy-start | bytes 6291460
  101.2 23.7 %copy-start.37 = (s32[32]{0:T(128)S(1)}, s32[32]{0:T(128)}, u32[]{:S(2)}) copy-start(s32[32]{0:T(128)} %copy-done.35) | copy-start | bytes 388
  119.5 3.1 %collective-permute-start.6 = (f32[64,128]{1,0:T(8,128)}, f32[64,128]{1,0:T(8,128)S(1)}, u32[]{:S(2)}, u32[]{:S(2)}) collective-permute-start(f32[64,128]{1,0:T(8,128)} %get-tuple-element.84.values.start), channel_id=1, source_target_pairs={{0,1},{1,2},{2,3},{3,4},{4,5},{5,6},{6,7},{7,8},{8,9},{9,10},{10,1... | collective-permute-start | bytes 98312 | tf_op jit(solution)/shard_map/ppermute | solution.py:570
  121.3 3.6 %collective-permute-start.7 = (f32[64,128]{1,0:T(8,128)}, f32[64,128]{1,0:T(8,128)S(1)}, u32[]{:S(2)}, u32[]{:S(2)}) collective-permute-start(f32[64,128]{1,0:T(8,128)} %get-tuple-element.82), channel_id=1, source_target_pairs={{1,0},{2,1},{3,2},{4,3},{5,4},{6,5},{7,6},{8,7},{9,8},{10,9},{11,1... | collective-permute-start | bytes 98312 | tf_op jit(solution)/shard_map/ppermute | solution.py:574
  128.3 9.3 %collective-permute-start.8 = (f32[64,128]{1,0:T(8,128)S(1)}, f32[64,128]{1,0:T(8,128)S(1)}, u32[]{:S(2)}, u32[]{:S(2)}) collective-permute-start(f32[64,128]{1,0:T(8,128)S(1)} %shard_map.158.image), channel_id=1, source_target_pairs={{0,1},{1,2},{2,3},{3,4},{4,5},{5,6},{6,7},{7,8},{8,9},{9,10},{10,1... | collective-permute-start | bytes 98312 | tf_op jit(solution)/shard_map/ppermute | solution.py:570
  141.9 22.7 %all-to-all-start.3 = ((f32[128,1,128]{2,1,0:T(1,128)}), f32[128,1,128]{2,1,0:T(1,128)S(1)}, u32[]{:S(2)}, u32[]{:S(2)}) async-start(f32[128,1,128]{2,1,0:T(1,128)} %bitcast.21), calls=%async_computation.3 | async-start | bytes 131072 | tf_op jit(solution)/shard_map/all_to_all | solution.py:566
  163.8 25.0 %copy-start.42 = (f32[8,128]{1,0:T(8,128)S(1)}, f32[8,128]{1,0:T(8,128)}, u32[]{:S(2)}) copy-start(f32[8,128]{1,0:T(8,128)} %get-tuple-element.66.slot_row) | copy-start | bytes 12292
  165.8 37.9 %copy-start.21 = (f32[40,128]{1,0:T(8,128)S(1)}, f32[40,128]{1,0:T(8,128)}, u32[]{:S(2)}) copy-start(f32[40,128]{1,0:T(8,128)} %copy-done.20) | copy-start | bytes 61444
  165.8 37.9 %copy-start.23 = (f32[40,128]{1,0:T(8,128)S(1)}, f32[40,128]{1,0:T(8,128)}, u32[]{:S(2)}) copy-start(f32[40,128]{1,0:T(8,128)} %copy-done.22) | copy-start | bytes 61444
  165.8 37.9 %copy-start.25 = (f32[40,128]{1,0:T(8,128)S(1)}, f32[40,128]{1,0:T(8,128)}, u32[]{:S(2)}) copy-start(f32[40,128]{1,0:T(8,128)} %copy-done.24) | copy-start | bytes 61444
  165.8 37.9 %copy-start.27 = (f32[40,128]{1,0:T(8,128)S(1)}, f32[40,128]{1,0:T(8,128)}, u32[]{:S(2)}) copy-start(f32[40,128]{1,0:T(8,128)} %copy-done.26) | copy-start | bytes 61444
  169.6 19.2 %all-to-all-start.4 = ((f32[128,2,128]{2,1,0:T(2,128)}), f32[128,2,128]{2,1,0:T(2,128)}, u32[]{:S(2)}, u32[]{:S(2)}) async-start(f32[128,2,128]{2,1,0:T(2,128)} %bitcast.66), calls=%async_computation.4 | async-start | bytes 262144 | tf_op jit(solution)/shard_map/all_to_all | solution.py:566
  182.1 25.0 %collective-permute-start.10 = (f32[64,128]{1,0:T(8,128)}, f32[64,128]{1,0:T(8,128)}, u32[]{:S(2)}, u32[]{:S(2)}) collective-permute-start(f32[64,128]{1,0:T(8,128)} %shard_map.165), channel_id=1, source_target_pairs={{1,0},{2,1},{3,2},{4,3},{5,4},{6,5},{7,6},{8,7},{9,8},{10,9},{11,1... | collective-permute-start | bytes 98312 | tf_op jit(solution)/shard_map/ppermute | solution.py:574
  183.2 23.9 %collective-permute-start.9 = (f32[64,128]{1,0:T(8,128)}, f32[64,128]{1,0:T(8,128)}, u32[]{:S(2)}, u32[]{:S(2)}) collective-permute-start(f32[64,128]{1,0:T(8,128)} %get-tuple-element.101.values.field), channel_id=1, source_target_pairs={{0,1},{1,2},{2,3},{3,4},{4,5},{5,6},{6,7},{7,8},{8,9},{9,10},{10,1... | collective-permute-start | bytes 98312 | tf_op jit(solution)/shard_map/ppermute | solution.py:570
  193.8 19.5 %all-to-all-start.5 = ((f32[128,2,128]{2,1,0:T(2,128)}), f32[128,2,128]{2,1,0:T(2,128)}, u32[]{:S(2)}, u32[]{:S(2)}) async-start(f32[128,2,128]{2,1,0:T(2,128)} %bitcast.54), calls=%async_computation.5 | async-start | bytes 262144 | tf_op jit(solution)/shard_map/all_to_all | solution.py:566
  213.3 23.2 %copy-start.2 = (f32[8,4,128,128]{3,2,1,0:T(8,128)S(1)}, f32[8,4,128,128]{3,2,1,0:T(8,128)}, u32[]{:S(2)}) copy-start(f32[8,4,128,128]{3,2,1,0:T(8,128)} %couplings.19) | copy-start | bytes 6291460
  213.3 23.2 %copy-start.38 = (s32[32]{0:T(128)S(1)}, s32[32]{0:T(128)}, u32[]{:S(2)}) copy-start(s32[32]{0:T(128)} %copy-done.35) | copy-start | bytes 388
  213.3 26.7 %copy-start.7 = (f32[5,8,128,128]{3,2,1,0:T(8,128)S(1)}, f32[5,8,128,128]{3,2,1,0:T(8,128)}, u32[]{:S(2)}) copy-start(f32[5,8,128,128]{3,2,1,0:T(8,128)} %state.9) | copy-start | bytes 7864324
  232.0 2.3 collective-permute-start.11
  232.9 13.2 %copy-start.12 = (f32[8,64,128]{2,1,0:T(8,128)S(1)}, f32[8,64,128]{2,1,0:T(8,128)}, u32[]{:S(2)}) copy-start(f32[8,64,128]{2,1,0:T(8,128)} %pad_bitcast_fusion.tested) | copy-start | bytes 786436
  232.9 3.6 %collective-permute-start.12 = (f32[64,128]{1,0:T(8,128)}, f32[64,128]{1,0:T(8,128)S(1)}, u32[]{:S(2)}, u32[]{:S(2)}) collective-permute-start(f32[64,128]{1,0:T(8,128)} %get-tuple-element.103), channel_id=1, source_target_pairs={{1,0},{2,1},{3,2},{4,3},{5,4},{6,5},{7,6},{8,7},{9,8},{10,9},{11,1... | collective-permute-start | bytes 98312 | tf_op jit(solution)/shard_map/ppermute | solution.py:574
  239.8 22.1 %copy-start.29 = (f32[5,128,128]{2,1,0:T(8,128)S(1)}, f32[5,128,128]{2,1,0:T(8,128)}, u32[]{:S(2)}) copy-start(f32[5,128,128]{2,1,0:T(8,128)} %copy-done.28) | copy-start | bytes 983044
  239.9 6.3 %collective-permute-start.13 = (f32[64,128]{1,0:T(8,128)S(1)}, f32[64,128]{1,0:T(8,128)S(1)}, u32[]{:S(2)}, u32[]{:S(2)}) collective-permute-start(f32[64,128]{1,0:T(8,128)S(1)} %shard_map.168.image), channel_id=1, source_target_pairs={{0,1},{1,2},{2,3},{3,4},{4,5},{5,6},{6,7},{7,8},{8,9},{9,10},{10,1... | collective-permute-start | bytes 98312 | tf_op jit(solution)/shard_map/ppermute | solution.py:570
  249.6 21.8 %all-to-all-start.6 = ((f32[128,1,128]{2,1,0:T(1,128)}), f32[128,1,128]{2,1,0:T(1,128)S(1)}, u32[]{:S(2)}, u32[]{:S(2)}) async-start(f32[128,1,128]{2,1,0:T(1,128)} %bitcast.29), calls=%async_computation.6 | async-start | bytes 131072 | tf_op jit(solution)/shard_map/all_to_all | solution.py:566
  (29 other events, 125.4 us)

commit v2 on v1

--- a/solution.py
+++ b/solution.py
@@ -696,9 +696,11 @@
         return call(back_kernel, shape(64, 128), scalars=1)(pattern, values, couplings)
 
     def applied(values, back, shift, gate=None):
-        before, behind = forward(values), backward(back)
+        before = forward(values)
         if gate is not None:
+            back, before = lax.optimization_barrier((back, before))
             values = lax.optimization_barrier((values, gate))[0]
+        behind = backward(back)
         return call(
             functools.partial(apply_kernel, shift),
             shape(64, 128),
@@ -739,8 +741,6 @@
         ready = lax.optimization_barrier((field, motion))[0]
         stiff = applied(ready, back_of(ready), 0.0, sent)
         base = load - stiff
-        fluid_parts.append(fluid((1, 2, 3) if count == 0 else (4,), sent))
-        amounts, fluid_parts[-1] = lax.optimization_barrier((amounts, fluid_parts[-1]))
         start, back = find_loads(support, pattern, amounts, geo, phi, base, couplings)
         image = applied(start, back, SHIFT)
         ahead = forward(image)
@@ -748,7 +748,7 @@
             first_half = basis_motion(0, support, geo, field, start, image, responses, phi)
             ahead, first_half = lax.optimization_barrier((ahead, first_half))
         else:
-            fluid_parts.append(fluid((5, 6, 7), image))
+            fluid_parts.append(fluid((4, 5, 6, 7), image))
             ahead, fluid_parts[-1] = lax.optimization_barrier((ahead, fluid_parts[-1]))
         row = call(
             sums_kernel,
@@ -773,6 +773,9 @@
                 1, support, geo, field, gated[0], gated[1], responses, phi
             )
             totals, final_half = lax.optimization_barrier((totals, final_half))
+        else:
+            fluid_parts.insert(0, fluid((1, 2, 3), row))
+            totals, fluid_parts[0] = lax.optimization_barrier((totals, fluid_parts[0]))
         solve = functools.partial(solve_kernel, count)
         if count == 0:
             outs = [shape(64, 128)] * 3 + [shape(16, 128), shape(256, 128)]

time: 275 us -> 270 us (0.982)
  waiting for transfers between devices: 29.9 us -> 24.9 us
  Pallas kernels: 134 us -> 130 us
    all_to_all x7, starting transfers between devices: 71.2 us -> 60.1 us  [exchange(): return lax.all_to_all(values, AXES, split_axis=0, concat_axis=0, tiled=True)]
    ppermute x4, starting transfers between devices: 1.19 us -> 12.1 us  [backward(): lax.ppermute(values, AXES, [((i + 1) % DEVICES, i) for i in range(DEVICES)])]
    all_to_all x7, waiting for transfers between devices: 21.9 us -> 18.3 us  [exchange(): return lax.all_to_all(values, AXES, split_axis=0, concat_axis=0, tiled=True)]
    pallas_call x19 -> x18, Pallas kernels: 50.3 us -> 46.7 us  [run(): pl.pallas_call(kernel, out_shape=outs, in_specs=specs + [pl.BlockSpec()]...]
    unnamed x117 -> x127, local copies, waits for them, and re-layouts: 15.7 us -> 17.8 us
  transfers between devices with their start and end apart: 21 -> 21, of which waited for: 11 -> 9; matrix products, arithmetic and copies ran while one was open for 3% -> 2% of each run, Pallas kernels for 27% -> 27%
where the time goes in v2:
time: 270 us; the launch traced here: 269 us
  Pallas kernels  130 us (48%)
  starting transfers between devices  84.7 us (31%)
  waiting for transfers between devices  24.9 us (9%)
  local copies, waits for them, and re-layouts  21.9 us (8%)
  other arithmetic  5.41 us (2%)
    pallas_call x5, Pallas kernels, whole(): pl.pallas_call(kernel, out_shape=outs, in_specs=[pl.BlockSpec(memory_spac...  83.3 us
    all_to_all x7, starting transfers between devices, exchange(): return lax.all_to_all(values, AXES, split_axis=0, concat_axis=0, tiled=True)  60.1 us
    pallas_call x18, Pallas kernels, run(): pl.pallas_call(kernel, out_shape=outs, in_specs=specs + [pl.BlockSpec()]...  46.7 us
    all_to_all x7, waiting for transfers between devices, exchange(): return lax.all_to_all(values, AXES, split_axis=0, concat_axis=0, tiled=True)  18.3 us
    unnamed x127, local copies, waits for them, and re-layouts  17.8 us
    ppermute x4, starting transfers between devices, backward(): lax.ppermute(values, AXES, [((i + 1) % DEVICES, i) for i in range(DEVICES)])  12.1 us
    ppermute x4, starting transfers between devices, shift(): lax.ppermute(values, axis, [(i, (i + step) % count) for i in range(count)])  7.33 us
  transfers between devices with their start and end apart: 21, of which 9 were waited for; matrix products, arithmetic and copies ran while one was open for 2% of the time, Pallas kernels for 27%

profile of v2, /device:TPU:1, one launch (start us, length us, event | category | flops | bytes accessed | tf_op | source)
XLA Modules:
  0.0 268.6 jit_solution(6551261803776959492)
XLA Ops:
  0.7 2.8 %shard_map.148 = (f32[2048,128]{1,0:T(8,128)}, f32[8,128]{1,0:T(8,128)}, f32[128,128]{1,0:T(8,128)}) custom-call(s32[1,128]{1,0:T(1,128)} %bitcast.72, f32[3,128,128]{2,1,0:T(8,128)} %bitcast.67, f32[3,128,128]{2,1,0:T(8,128)} %bitcast.68, s32[2,128]{1,0:T(2,128)} %bitcast.71), custom_call_target="tpu_custom_call" | custom-call | tf_op jit(solution)/shard_map/pallas_call | solution.py:551
  3.4 11.5 %all-to-all-start = ((f32[128,16,128]{2,1,0:T(8,128)}), f32[128,16,128]{2,1,0:T(8,128)S(1)}, u32[]{:S(2)}, u32[]{:S(2)}) async-start(f32[128,16,128]{2,1,0:T(8,128)} %bitcast.63), calls=%async_computation | async-start | bytes 2097152 | tf_op jit(solution)/shard_map/all_to_all | solution.py:566
  15.0 1.7 copy-done.3
  16.7 1.7 shard_map.149
  18.4 1.6 collective-permute-start
  20.0 4.0 %collective-permute-start.1 = (f32[40,128]{1,0:T(8,128)S(1)}, f32[40,128]{1,0:T(8,128)S(1)}, u32[]{:S(2)}, u32[]{:S(2)}) collective-permute-start(f32[40,128]{1,0:T(8,128)S(1)} %get-tuple-element.59), channel_id=1, source_target_pairs={{0,120},{8,0},{16,8},{24,16},{32,24},{40,32},{48,40},{56,48},{64,5... | collective-permute-start | bytes 61448 | tf_op jit(solution)/shard_map/ppermute | solution.py:579
  24.0 1.8 collective-permute-start.2
  28.2 1.0 slice_bitcast_fusion.bottom
  29.2 4.9 %all-to-all-done = f32[128,16,128]{2,1,0:T(8,128)S(1)} async-done(((f32[128,16,128]{2,1,0:T(8,128)}), f32[128,16,128]{2,1,0:T(8,128)S(1)}, u32[]{:S(2)}, u32[]{:S(2)}) %all-to-all-start) | async-done | bytes 1048608 | tf_op jit(solution)/shard_map/all_to_all | solution.py:566
  35.1 28.8 %shard_map.151 = (bf16[256,256,256]{2,1,0:T(8,128)(2,1)}, f32[256,128]{1,0:T(8,128)}) custom-call(s32[512]{0:T(512)} %reshape.51.support, f32[2048,128]{1,0:T(8,128)} %bitcast.58, bf16[16,128,64]{2,1,0:T(8,128)(2,1)} %copy-done.15, f32[64,128]{1,0:T(8,128)} %pad_bitcast_fusion.3.field.values.extra.last), custom_call_target="tpu_custom_call" | custom-call | flops 2000000000 | bytes 40000000 | tf_op jit(solution)/shard_map/pallas_call | solution.py:590
  64.0 4.6 %all-to-all-start.1 = ((f32[128,2,128]{2,1,0:T(2,128)}), f32[128,2,128]{2,1,0:T(2,128)S(1)}, u32[]{:S(2)}, u32[]{:S(2)}) async-start(f32[128,2,128]{2,1,0:T(2,128)} %bitcast.69), calls=%async_computation.1 | async-start | bytes 262144 | tf_op jit(solution)/shard_map/all_to_all | solution.py:566
  68.6 1.7 collective-permute-start.4
  70.5 2.0 shard_map.154
  72.6 6.6 %collective-permute-start.5 = (f32[64,128]{1,0:T(8,128)S(1)}, f32[64,128]{1,0:T(8,128)S(1)}, u32[]{:S(2)}, u32[]{:S(2)}) collective-permute-start(f32[64,128]{1,0:T(8,128)S(1)} %shard_map.154), channel_id=1, source_target_pairs={{1,0},{2,1},{3,2},{4,3},{5,4},{6,5},{7,6},{8,7},{9,8},{10,9},{11,1... | collective-permute-start | bytes 98312 | tf_op jit(solution)/shard_map/ppermute | solution.py:574
  79.3 1.7 copy-done.4
  81.0 1.5 shard_map.152
  82.5 1.5 shard_map.153
  84.0 3.5 %all-to-all-start.2 = ((f32[128,2,128]{2,1,0:T(2,128)}), f32[128,2,128]{2,1,0:T(2,128)S(1)}, u32[]{:S(2)}, u32[]{:S(2)}) async-start(f32[128,2,128]{2,1,0:T(2,128)} %bitcast.12), calls=%async_computation.2 | async-start | bytes 262144 | tf_op jit(solution)/shard_map/all_to_all | solution.py:566
  87.6 2.6 shard_map.155
  90.8 6.8 %all-to-all-done.2 = f32[128,2,128]{2,1,0:T(2,128)S(1)} async-done(((f32[128,2,128]{2,1,0:T(2,128)}), f32[128,2,128]{2,1,0:T(2,128)S(1)}, u32[]{:S(2)}, u32[]{:S(2)}) %all-to-all-start.2) | async-done | bytes 131104 | tf_op jit(solution)/shard_map/all_to_all | solution.py:566
  98.3 18.3 %shard_map.156 = (f32[64,128]{1,0:T(8,128)}, f32[64,128]{1,0:T(8,128)}) custom-call(s32[512]{0:T(512)} %reshape.51.support, s32[32]{0:T(128)} %copy-done.39, f32[256,128]{1,0:T(8,128)} %bitcast.65, f32[2048,128]{1,0:T(8,128)} %bitcast.59, bf16[256,256,256]{2,1,0:T(8,128)(2,1)} %get-tuple-element.71.phi_hbm, f32[64,128]{1,0:T(8,128)} %fusion.2.base, ...), custom_call_target="tpu_custom_call" | custom-call | flops 2000000000 | bytes 40000000 | tf_op jit(solution)/shard_map/pallas_call | solution.py:590
  118.6 2.2 collective-permute-done.7.behind
  121.6 2.6 shard_map.157.image
  124.8 8.8 %shard_map.158.more_0_ = f32[128,16,128]{2,1,0:T(8,128)} custom-call(s32[512]{0:T(512)} %reshape.51.support, f32[2048,128]{1,0:T(8,128)} %bitcast.60, f32[64,128]{1,0:T(8,128)} %pad_bitcast_fusion.3.field.values.extra.last, f32[64,128]{1,0:T(8,128)} %get-tuple-element.79.values.start, f32[64,128]{1,0:T(8,128)} %copy-done.13, ...), custom_call_target="tpu_custom_call" | custom-call | flops 2000000000 | bytes 40000000 | tf_op jit(solution)/shard_map/pallas_call | solution.py:590
  134.4 3.5 %shard_map.159 = f32[128,128]{1,0:T(8,128)} custom-call(s32[32]{0:T(128)S(1)} %copy-done.40, f32[64,128]{1,0:T(8,128)S(1)} %copy-done.12, f32[64,128]{1,0:T(8,128)S(1)} %copy-done.14, f32[64,128]{1,0:T(8,128)S(1)} %collective-permute-done.8.before, f32[64,128]{1,0:T(8,128)S(1)} %pad_bitcast_fusion.4.diagonal, f32[8,4,128,128]{3,2,1,0:T(8,128)S(1)} %copy-done.1, ...), custom_call_target="tpu_custom_call" | custom-call | tf_op jit(solution)/shard_map/pallas_call | solution.py:551
  137.9 13.4 %all-to-all-start.3 = ((f32[128,1,128]{2,1,0:T(1,128)}), f32[128,1,128]{2,1,0:T(1,128)S(1)}, u32[]{:S(2)}, u32[]{:S(2)}) async-start(f32[128,1,128]{2,1,0:T(1,128)} %bitcast.21), calls=%async_computation.3 | async-start | bytes 131072 | tf_op jit(solution)/shard_map/all_to_all | solution.py:566
  151.3 8.8 %shard_map.160.more_1_ = f32[128,16,128]{2,1,0:T(8,128)} custom-call(s32[512]{0:T(512)} %reshape.51.support, f32[2048,128]{1,0:T(8,128)} %bitcast.61, f32[64,128]{1,0:T(8,128)} %pad_bitcast_fusion.3.field.values.extra.last, f32[64,128]{1,0:T(8,128)} %get-tuple-element.79.values.start, f32[64,128]{1,0:T(8,128)} %copy-done.13, ...), custom_call_target="tpu_custom_call" | custom-call | flops 2000000000 | bytes 40000000 | tf_op jit(solution)/shard_map/pallas_call | solution.py:590
  161.4 3.8 %shard_map.161 = (f32[64,128]{1,0:T(8,128)}, f32[64,128]{1,0:T(8,128)}, f32[64,128]{1,0:T(8,128)}, f32[16,128]{1,0:T(8,128)}, f32[256,128]{1,0:T(8,128)}) custom-call(f32[128,128]{1,0:T(8,128)} %bitcast.66, f32[16,128]{1,0:T(8,128)} %broadcast_in_dim.16.memory, f32[64,128]{1,0:T(8,128)} %pad_bitcast_fusion.3.field.values.extra.last, ...), custom_call_target="tpu_custom_call" | custom-call | tf_op jit(solution)/shard_map/pallas_call | solution.py:551
  165.2 9.0 %all-to-all-start.4 = ((f32[128,2,128]{2,1,0:T(2,128)}), f32[128,2,128]{2,1,0:T(2,128)S(1)}, u32[]{:S(2)}, u32[]{:S(2)}) async-start(f32[128,2,128]{2,1,0:T(2,128)} %bitcast.70), calls=%async_computation.4 | async-start | bytes 262144 | tf_op jit(solution)/shard_map/all_to_all | solution.py:566
  174.2 1.7 collective-permute-start.9
  176.7 2.7 shard_map.163
  180.0 5.4 %collective-permute-start.10 = (f32[64,128]{1,0:T(8,128)}, f32[64,128]{1,0:T(8,128)}, u32[]{:S(2)}, u32[]{:S(2)}) collective-permute-start(f32[64,128]{1,0:T(8,128)} %shard_map.163), channel_id=1, source_target_pairs={{1,0},{2,1},{3,2},{4,3},{5,4},{6,5},{7,6},{8,7},{9,8},{10,9},{11,1... | collective-permute-start | bytes 98312 | tf_op jit(solution)/shard_map/ppermute | solution.py:574
  187.7 4.5 %all-to-all-start.5 = ((f32[128,2,128]{2,1,0:T(2,128)}), f32[128,2,128]{2,1,0:T(2,128)S(1)}, u32[]{:S(2)}, u32[]{:S(2)}) async-start(f32[128,2,128]{2,1,0:T(2,128)} %bitcast.56), calls=%async_computation.5 | async-start | bytes 262144 | tf_op jit(solution)/shard_map/all_to_all | solution.py:566
  193.0 2.8 %shard_map.164 = f32[64,128]{1,0:T(8,128)S(1)} custom-call(s32[32]{0:T(128)S(1)} %copy-done.40, f32[64,128]{1,0:T(8,128)S(1)} %copy-done.17, f32[64,128]{1,0:T(8,128)S(1)} %copy-done.44, f32[64,128]{1,0:T(8,128)} %collective-permute-done.10.behind, f32[64,128]{1,0:T(8,128)S(1)} %pad_bitcast_fusion.4.diagonal, f32[8,4,128,128]{3,2,1,0:T(8,128)S(1)} %copy-done.1), custom_call_target="tpu_custom_call" | custom-call | tf_op jit(solution)/shard_map/pallas_call | solution.py:551
  195.9 1.3 fusion.1.base
  197.2 5.1 %all-to-all-done.5 = f32[128,2,128]{2,1,0:T(2,128)S(1)} async-done(((f32[128,2,128]{2,1,0:T(2,128)}), f32[128,2,128]{2,1,0:T(2,128)S(1)}, u32[]{:S(2)}, u32[]{:S(2)}) %all-to-all-start.5) | async-done | bytes 131104 | tf_op jit(solution)/shard_map/all_to_all | solution.py:566
  203.0 18.6 %shard_map.165 = (f32[64,128]{1,0:T(8,128)}, f32[64,128]{1,0:T(8,128)}) custom-call(s32[512]{0:T(512)} %reshape.51.support, s32[32]{0:T(128)} %copy-done.39, f32[256,128]{1,0:T(8,128)} %bitcast.64, f32[2048,128]{1,0:T(8,128)} %bitcast.62, bf16[256,256,256]{2,1,0:T(8,128)(2,1)} %get-tuple-element.71.phi_hbm, f32[64,128]{1,0:T(8,128)} %fusion.1.base, ...), custom_call_target="tpu_custom_call" | custom-call | flops 2000000000 | bytes 40000000 | tf_op jit(solution)/shard_map/pallas_call | solution.py:590
  222.4 1.3 collective-permute-done.11.before
  223.7 2.2 collective-permute-done.12.behind
  226.7 2.6 shard_map.166.image
  229.5 6.2 %shard_map.167 = f32[5,4,128,128]{3,2,1,0:T(8,128)S(1)} custom-call(f32[5,8,128,128]{3,2,1,0:T(8,128)S(1)} %copy-done.5, f32[40,128]{1,0:T(8,128)S(1)} %copy-done.27, f32[40,128]{1,0:T(8,128)S(1)} %copy-done.30, f32[40,128]{1,0:T(8,128)S(1)} %copy-done.33, f32[40,128]{1,0:T(8,128)S(1)} %copy-done.36), custom_call_target="tpu_custom_call" | custom-call | flops 160000000 | bytes 2800000 | tf_op jit(solution)/shard_map/pallas_call | solution.py:551
  235.8 1.1 copy-done.7
  236.9 2.8 %shard_map.168 = f32[128,128]{1,0:T(8,128)S(1)} custom-call(s32[32]{0:T(128)S(1)} %copy-done.41, f32[64,128]{1,0:T(8,128)S(1)} %copy-done.19, f32[64,128]{1,0:T(8,128)S(1)} %shard_map.166.image, f32[64,128]{1,0:T(8,128)S(1)} %collective-permute-done.13.before, f32[64,128]{1,0:T(8,128)S(1)} %pad_bitcast_fusion.4.diagonal, f32[8,4,128,128]{3,2,1,0:T(8,128)S(1)} %copy-done.2, ...), custom_call_target="tpu_custom_call" | custom-call | tf_op jit(solution)/shard_map/pallas_call | solution.py:551
  240.4 13.6 %all-to-all-start.6 = ((f32[128,1,128]{2,1,0:T(1,128)}), f32[128,1,128]{2,1,0:T(1,128)S(1)}, u32[]{:S(2)}, u32[]{:S(2)}) async-start(f32[128,1,128]{2,1,0:T(1,128)} %bitcast.55), calls=%async_computation.6 | async-start | bytes 131072 | tf_op jit(solution)/shard_map/all_to_all | solution.py:566
  257.0 4.8 %shard_map.169 = f32[5,3,128,128]{3,2,1,0:T(8,128)S(1)} custom-call(f32[5,8,128,128]{3,2,1,0:T(8,128)S(1)} %copy-done.5, f32[40,128]{1,0:T(8,128)S(1)} %copy-done.28, f32[40,128]{1,0:T(8,128)S(1)} %copy-done.31, f32[40,128]{1,0:T(8,128)S(1)} %copy-done.34, f32[40,128]{1,0:T(8,128)S(1)} %copy-done.37), custom_call_target="tpu_custom_call" | custom-call | flops 120000000 | bytes 2100000 | tf_op jit(solution)/shard_map/pallas_call | solution.py:551
  261.8 0.9 copy-done.8
  263.5 1.7 shard_map.170
  265.2 3.4 %pad_maximum_fusion = f32[5,8,128,128]{3,2,1,0:T(8,128)} fusion(f32[5,4,128,128]{3,2,1,0:T(8,128)} %copy-done.7, f32[5,3,128,128]{3,2,1,0:T(8,128)} %copy-done.8, f32[5,1,128,128]{3,2,1,0:T(8,128)S(1)} %bitcast.53), kind=kLoop, calls=%fused_computation | loop fusion | flops 1310720 | bytes 5242880 | tf_op jit(solution)/shard_map/concatenate | solution.py:798
  (161 shorter events, 21.5 us)
Async XLA Ops:
  0.6 25.1 %copy-start.57 = (f32[8,3,128]{2,0,1:T(8,128)S(1)}, f32[8,3,128]{2,0,1:T(8,128)}, u32[]{:S(2)}) copy-start(f32[8,3,128]{2,0,1:T(8,128)} %param.23) | copy-start | bytes 36868
  0.6 25.1 %copy-start.47 = (f32[8,3,128]{2,0,1:T(8,128)S(1)}, f32[8,3,128]{2,0,1:T(8,128)}, u32[]{:S(2)}) copy-start(f32[8,3,128]{2,0,1:T(8,128)} %param.18) | copy-start | bytes 36868
  3.4 23.4 %copy-start.56 = (f32[8,8,3,128]{3,1,2,0:T(8,128)S(1)}, f32[8,8,3,128]{3,1,2,0:T(8,128)}, u32[]{:S(2)}) copy-start(f32[8,8,3,128]{3,1,2,0:T(8,128)} %param.25) | copy-start | bytes 294916
  3.4 23.4 %copy-start.52 = (f32[8,8,3,128]{3,1,2,0:T(8,128)S(1)}, f32[8,8,3,128]{3,1,2,0:T(8,128)}, u32[]{:S(2)}) copy-start(f32[8,8,3,128]{3,1,2,0:T(8,128)} %param.24) | copy-start | bytes 294916
  3.4 30.7 %all-to-all-start = ((f32[128,16,128]{2,1,0:T(8,128)}), f32[128,16,128]{2,1,0:T(8,128)S(1)}, u32[]{:S(2)}, u32[]{:S(2)}) async-start(f32[128,16,128]{2,1,0:T(8,128)} %bitcast.63), calls=%async_computation | async-start | bytes 2097152 | tf_op jit(solution)/shard_map/all_to_all | solution.py:566
  18.4 45.5 %collective-permute-start = (f32[40,128]{1,0:T(8,128)S(1)}, f32[40,128]{1,0:T(8,128)S(1)}, u32[]{:S(2)}, u32[]{:S(2)}) collective-permute-start(f32[40,128]{1,0:T(8,128)S(1)} %get-tuple-element.58), channel_id=1, source_target_pairs={{0,8},{8,16},{16,24},{24,32},{32,40},{40,48},{48,56},{56,64},{64,7... | collective-permute-start | bytes 61448 | tf_op jit(solution)/shard_map/ppermute | solution.py:579
  20.0 44.0 %collective-permute-start.1 = (f32[40,128]{1,0:T(8,128)S(1)}, f32[40,128]{1,0:T(8,128)S(1)}, u32[]{:S(2)}, u32[]{:S(2)}) collective-permute-start(f32[40,128]{1,0:T(8,128)S(1)} %get-tuple-element.59), channel_id=1, source_target_pairs={{0,120},{8,0},{16,8},{24,16},{32,24},{40,32},{48,40},{56,48},{64,5... | collective-permute-start | bytes 61448 | tf_op jit(solution)/shard_map/ppermute | solution.py:579
  24.0 40.0 %collective-permute-start.2 = (f32[40,128]{1,0:T(8,128)S(1)}, f32[40,128]{1,0:T(8,128)S(1)}, u32[]{:S(2)}, u32[]{:S(2)}) collective-permute-start(f32[40,128]{1,0:T(8,128)S(1)} %get-tuple-element.60), channel_id=1, source_target_pairs={{0,1},{1,2},{2,3},{3,4},{4,5},{5,6},{6,7},{7,0},{8,9},{9,10},{10,1... | collective-permute-start | bytes 61448 | tf_op jit(solution)/shard_map/ppermute | solution.py:579
  25.8 38.2 %collective-permute-start.3 = (f32[40,128]{1,0:T(8,128)S(1)}, f32[40,128]{1,0:T(8,128)S(1)}, u32[]{:S(2)}, u32[]{:S(2)}) collective-permute-start(f32[40,128]{1,0:T(8,128)S(1)} %get-tuple-element.61), channel_id=1, source_target_pairs={{0,7},{1,0},{2,1},{3,2},{4,3},{5,4},{6,5},{7,6},{8,15},{9,8},{10,9... | collective-permute-start | bytes 61448 | tf_op jit(solution)/shard_map/ppermute | solution.py:579
  35.1 33.5 %copy-start.9 = (f32[64,128]{1,0:T(8,128)S(1)}, f32[64,128]{1,0:T(8,128)}, u32[]{:S(2)}) copy-start(f32[64,128]{1,0:T(8,128)} %pad_bitcast_fusion.3.field.values.extra.last) | copy-start | bytes 98308
  35.1 35.2 %copy-start.60 = (s32[8,4]{0,1:T(4,128)S(1)}, s32[8,4]{0,1:T(4,128)}, u32[]{:S(2)}) copy-start(s32[8,4]{0,1:T(4,128)} %param.20) | copy-start | bytes 388
  35.1 35.4 %copy-start = (f32[8,4,128,128]{3,2,1,0:T(8,128)S(1)}, f32[8,4,128,128]{3,2,1,0:T(8,128)}, u32[]{:S(2)}) copy-start(f32[8,4,128,128]{3,2,1,0:T(8,128)} %couplings.19) | copy-start | bytes 6291460
  63.9 18.5 %copy-start.26 = (f32[40,128]{1,0:T(8,128)}, f32[40,128]{1,0:T(8,128)S(1)}, u32[]{:S(2)}) copy-start(f32[40,128]{1,0:T(8,128)S(1)} %collective-permute-done.low_x) | copy-start | bytes 61444
  64.0 18.5 %copy-start.29 = (f32[40,128]{1,0:T(8,128)}, f32[40,128]{1,0:T(8,128)S(1)}, u32[]{:S(2)}) copy-start(f32[40,128]{1,0:T(8,128)S(1)} %collective-permute-done.1.high_x) | copy-start | bytes 61444
  64.0 18.5 %copy-start.32 = (f32[40,128]{1,0:T(8,128)}, f32[40,128]{1,0:T(8,128)S(1)}, u32[]{:S(2)}) copy-start(f32[40,128]{1,0:T(8,128)S(1)} %collective-permute-done.2.low_y) | copy-start | bytes 61444
  64.0 18.5 %copy-start.35 = (f32[40,128]{1,0:T(8,128)}, f32[40,128]{1,0:T(8,128)S(1)}, u32[]{:S(2)}) copy-start(f32[40,128]{1,0:T(8,128)S(1)} %collective-permute-done.3.high_y) | copy-start | bytes 61444
  64.0 18.5 %all-to-all-start.1 = ((f32[128,2,128]{2,1,0:T(2,128)}), f32[128,2,128]{2,1,0:T(2,128)S(1)}, u32[]{:S(2)}, u32[]{:S(2)}) async-start(f32[128,2,128]{2,1,0:T(2,128)} %bitcast.69), calls=%async_computation.1 | async-start | bytes 262144 | tf_op jit(solution)/shard_map/all_to_all | solution.py:566
  68.6 4.0 %collective-permute-start.4 = (f32[64,128]{1,0:T(8,128)S(1)}, f32[64,128]{1,0:T(8,128)S(1)}, u32[]{:S(2)}, u32[]{:S(2)}) collective-permute-start(f32[64,128]{1,0:T(8,128)S(1)} %copy-done.9), channel_id=1, source_target_pairs={{0,1},{1,2},{2,3},{3,4},{4,5},{5,6},{6,7},{7,8},{8,9},{9,10},{10,1... | collective-permute-start | bytes 98312 | tf_op jit(solution)/shard_map/ppermute | solution.py:570
  72.6 15.0 %collective-permute-start.5 = (f32[64,128]{1,0:T(8,128)S(1)}, f32[64,128]{1,0:T(8,128)S(1)}, u32[]{:S(2)}, u32[]{:S(2)}) collective-permute-start(f32[64,128]{1,0:T(8,128)S(1)} %shard_map.154), channel_id=1, source_target_pairs={{1,0},{2,1},{3,2},{4,3},{5,4},{6,5},{7,6},{8,7},{9,8},{10,9},{11,1... | collective-permute-start | bytes 98312 | tf_op jit(solution)/shard_map/ppermute | solution.py:574
  84.0 13.6 %all-to-all-start.2 = ((f32[128,2,128]{2,1,0:T(2,128)}), f32[128,2,128]{2,1,0:T(2,128)S(1)}, u32[]{:S(2)}, u32[]{:S(2)}) async-start(f32[128,2,128]{2,1,0:T(2,128)} %bitcast.12), calls=%async_computation.2 | async-start | bytes 262144 | tf_op jit(solution)/shard_map/all_to_all | solution.py:566
  98.3 19.0 %copy-start.53 = (f32[8,8,3,128]{3,1,2,0:T(8,128)S(1)}, f32[8,8,3,128]{3,1,2,0:T(8,128)}, u32[]{:S(2)}) copy-start(f32[8,8,3,128]{3,1,2,0:T(8,128)} %param.24) | copy-start | bytes 294916
  98.3 22.6 %copy-start.1 = (f32[8,4,128,128]{3,2,1,0:T(8,128)S(1)}, f32[8,4,128,128]{3,2,1,0:T(8,128)}, u32[]{:S(2)}) copy-start(f32[8,4,128,128]{3,2,1,0:T(8,128)} %couplings.19) | copy-start | bytes 6291460
  98.3 22.6 %copy-start.40 = (s32[32]{0:T(128)S(1)}, s32[32]{0:T(128)}, u32[]{:S(2)}) copy-start(s32[32]{0:T(128)} %copy-done.39) | copy-start | bytes 388
  116.6 2.1 collective-permute-start.6
  117.3 3.6 %collective-permute-start.7 = (f32[64,128]{1,0:T(8,128)}, f32[64,128]{1,0:T(8,128)S(1)}, u32[]{:S(2)}, u32[]{:S(2)}) collective-permute-start(f32[64,128]{1,0:T(8,128)} %get-tuple-element.77), channel_id=1, source_target_pairs={{1,0},{2,1},{3,2},{4,3},{5,4},{6,5},{7,6},{8,7},{9,8},{10,9},{11,1... | collective-permute-start | bytes 98312 | tf_op jit(solution)/shard_map/ppermute | solution.py:574
  124.3 9.4 %collective-permute-start.8 = (f32[64,128]{1,0:T(8,128)S(1)}, f32[64,128]{1,0:T(8,128)S(1)}, u32[]{:S(2)}, u32[]{:S(2)}) collective-permute-start(f32[64,128]{1,0:T(8,128)S(1)} %shard_map.157.image), channel_id=1, source_target_pairs={{0,1},{1,2},{2,3},{3,4},{4,5},{5,6},{6,7},{7,8},{8,9},{9,10},{10,1... | collective-permute-start | bytes 98312 | tf_op jit(solution)/shard_map/ppermute | solution.py:570
  137.9 22.8 %all-to-all-start.3 = ((f32[128,1,128]{2,1,0:T(1,128)}), f32[128,1,128]{2,1,0:T(1,128)S(1)}, u32[]{:S(2)}, u32[]{:S(2)}) async-start(f32[128,1,128]{2,1,0:T(1,128)} %bitcast.21), calls=%async_computation.3 | async-start | bytes 131072 | tf_op jit(solution)/shard_map/all_to_all | solution.py:566
  165.2 27.1 %copy-start.17 = (f32[64,128]{1,0:T(8,128)S(1)}, f32[64,128]{1,0:T(8,128)}, u32[]{:S(2)}) copy-start(f32[64,128]{1,0:T(8,128)} %get-tuple-element.89.values.field) | copy-start | bytes 98308
  165.2 20.2 %all-to-all-start.4 = ((f32[128,2,128]{2,1,0:T(2,128)}), f32[128,2,128]{2,1,0:T(2,128)S(1)}, u32[]{:S(2)}, u32[]{:S(2)}) async-start(f32[128,2,128]{2,1,0:T(2,128)} %bitcast.70), calls=%async_computation.4 | async-start | bytes 262144 | tf_op jit(solution)/shard_map/all_to_all | solution.py:566
  174.2 5.2 %collective-permute-start.9 = (f32[64,128]{1,0:T(8,128)}, f32[64,128]{1,0:T(8,128)S(1)}, u32[]{:S(2)}, u32[]{:S(2)}) collective-permute-start(f32[64,128]{1,0:T(8,128)} %get-tuple-element.89.values.field), channel_id=1, source_target_pairs={{0,1},{1,2},{2,3},{3,4},{4,5},{5,6},{6,7},{7,8},{8,9},{9,10},{10,1... | collective-permute-start | bytes 98312 | tf_op jit(solution)/shard_map/ppermute | solution.py:570
  180.0 12.3 %collective-permute-start.10 = (f32[64,128]{1,0:T(8,128)}, f32[64,128]{1,0:T(8,128)}, u32[]{:S(2)}, u32[]{:S(2)}) collective-permute-start(f32[64,128]{1,0:T(8,128)} %shard_map.163), channel_id=1, source_target_pairs={{1,0},{2,1},{3,2},{4,3},{5,4},{6,5},{7,6},{8,7},{9,8},{10,9},{11,1... | collective-permute-start | bytes 98312 | tf_op jit(solution)/shard_map/ppermute | solution.py:574
  187.7 14.6 %all-to-all-start.5 = ((f32[128,2,128]{2,1,0:T(2,128)}), f32[128,2,128]{2,1,0:T(2,128)S(1)}, u32[]{:S(2)}, u32[]{:S(2)}) async-start(f32[128,2,128]{2,1,0:T(2,128)} %bitcast.56), calls=%async_computation.5 | async-start | bytes 262144 | tf_op jit(solution)/shard_map/all_to_all | solution.py:566
  203.0 23.0 %copy-start.2 = (f32[8,4,128,128]{3,2,1,0:T(8,128)S(1)}, f32[8,4,128,128]{3,2,1,0:T(8,128)}, u32[]{:S(2)}) copy-start(f32[8,4,128,128]{3,2,1,0:T(8,128)} %couplings.19) | copy-start | bytes 6291460
  203.0 23.0 %copy-start.41 = (s32[32]{0:T(128)S(1)}, s32[32]{0:T(128)}, u32[]{:S(2)}) copy-start(s32[32]{0:T(128)} %copy-done.39) | copy-start | bytes 388
  203.0 26.5 %copy-start.5 = (f32[5,8,128,128]{3,2,1,0:T(8,128)S(1)}, f32[5,8,128,128]{3,2,1,0:T(8,128)}, u32[]{:S(2)}) copy-start(f32[5,8,128,128]{3,2,1,0:T(8,128)} %state.7) | copy-start | bytes 7864324
  203.0 26.5 %copy-start.27 = (f32[40,128]{1,0:T(8,128)S(1)}, f32[40,128]{1,0:T(8,128)}, u32[]{:S(2)}) copy-start(f32[40,128]{1,0:T(8,128)} %copy-done.26) | copy-start | bytes 61444
  203.0 26.5 %copy-start.30 = (f32[40,128]{1,0:T(8,128)S(1)}, f32[40,128]{1,0:T(8,128)}, u32[]{:S(2)}) copy-start(f32[40,128]{1,0:T(8,128)} %copy-done.29) | copy-start | bytes 61444
  203.0 26.5 %copy-start.33 = (f32[40,128]{1,0:T(8,128)S(1)}, f32[40,128]{1,0:T(8,128)}, u32[]{:S(2)}) copy-start(f32[40,128]{1,0:T(8,128)} %copy-done.32) | copy-start | bytes 61444
  203.0 26.5 %copy-start.36 = (f32[40,128]{1,0:T(8,128)S(1)}, f32[40,128]{1,0:T(8,128)}, u32[]{:S(2)}) copy-start(f32[40,128]{1,0:T(8,128)} %copy-done.35) | copy-start | bytes 61444
  221.7 2.1 collective-permute-start.11
  222.4 3.6 %collective-permute-start.12 = (f32[64,128]{1,0:T(8,128)}, f32[64,128]{1,0:T(8,128)S(1)}, u32[]{:S(2)}, u32[]{:S(2)}) collective-permute-start(f32[64,128]{1,0:T(8,128)} %get-tuple-element.93), channel_id=1, source_target_pairs={{1,0},{2,1},{3,2},{4,3},{5,4},{6,5},{7,6},{8,7},{9,8},{10,9},{11,1... | collective-permute-start | bytes 98312 | tf_op jit(solution)/shard_map/ppermute | solution.py:574
  229.3 7.5 %collective-permute-start.13 = (f32[64,128]{1,0:T(8,128)S(1)}, f32[64,128]{1,0:T(8,128)S(1)}, u32[]{:S(2)}, u32[]{:S(2)}) collective-permute-start(f32[64,128]{1,0:T(8,128)S(1)} %shard_map.166.image), channel_id=1, source_target_pairs={{0,1},{1,2},{2,3},{3,4},{4,5},{5,6},{6,7},{7,8},{8,9},{9,10},{10,1... | collective-permute-start | bytes 98312 | tf_op jit(solution)/shard_map/ppermute | solution.py:570
  236.9 26.6 %copy-start.6 = (f32[8,64,128]{2,1,0:T(8,128)S(1)}, f32[8,64,128]{2,1,0:T(8,128)}, u32[]{:S(2)}) copy-start(f32[8,64,128]{2,1,0:T(8,128)} %pad_bitcast_fusion.1.responses) | copy-start | bytes 786436
  236.9 26.6 %copy-start.48 = (f32[16,128]{1,0:T(8,128)S(1)}, f32[16,128]{1,0:T(8,128)}, u32[]{:S(2)}) copy-start(f32[16,128]{1,0:T(8,128)} %get-tuple-element.107.memory) | copy-start | bytes 24580
  240.4 23.1 %copy-start.20 = (f32[64,128]{1,0:T(8,128)S(1)}, f32[64,128]{1,0:T(8,128)}, u32[]{:S(2)}) copy-start(f32[64,128]{1,0:T(8,128)} %get-tuple-element.92.values.start) | copy-start | bytes 98308
  240.4 23.1 %copy-start.45 = (f32[64,128]{1,0:T(8,128)S(1)}, f32[64,128]{1,0:T(8,128)}, u32[]{:S(2)}) copy-start(f32[64,128]{1,0:T(8,128)} %get-tuple-element.108.last) | copy-start | bytes 98308
  240.4 23.1 %copy-start.22 = (f32[64,128]{1,0:T(8,128)S(1)}, f32[64,128]{1,0:T(8,128)}, u32[]{:S(2)}) copy-start(f32[64,128]{1,0:T(8,128)} %copy-done.21) | copy-start | bytes 98308
  240.4 23.1 %all-to-all-start.6 = ((f32[128,1,128]{2,1,0:T(1,128)}), f32[128,1,128]{2,1,0:T(1,128)S(1)}, u32[]{:S(2)}, u32[]{:S(2)}) async-start(f32[128,1,128]{2,1,0:T(1,128)} %bitcast.55), calls=%async_computation.6 | async-start | bytes 131072 | tf_op jit(solution)/shard_map/all_to_all | solution.py:566
  (34 other events, 149.8 us)

commit v3 on v2

--- a/solution.py
+++ b/solution.py
@@ -741,6 +741,9 @@
         ready = lax.optimization_barrier((field, motion))[0]
         stiff = applied(ready, back_of(ready), 0.0, sent)
         base = load - stiff
+        if count == 0:
+            fluid_parts.append(fluid((1, 2, 3), sent))
+            amounts, fluid_parts[0] = lax.optimization_barrier((amounts, fluid_parts[0]))
         start, back = find_loads(support, pattern, amounts, geo, phi, base, couplings)
         image = applied(start, back, SHIFT)
         ahead = forward(image)
@@ -773,9 +776,6 @@
                 1, support, geo, field, gated[0], gated[1], responses, phi
             )
             totals, final_half = lax.optimization_barrier((totals, final_half))
-        else:
-            fluid_parts.insert(0, fluid((1, 2, 3), row))
-            totals, fluid_parts[0] = lax.optimization_barrier((totals, fluid_parts[0]))
         solve = functools.partial(solve_kernel, count)
         if count == 0:
             outs = [shape(64, 128)] * 3 + [shape(16, 128), shape(256, 128)]

time: 270 us -> 273 us (1.011)
  starting transfers between devices: 84.7 us -> 88 us
    all_to_all x7, starting transfers between devices: 60.1 us -> 63.6 us  [exchange(): return lax.all_to_all(values, AXES, split_axis=0, concat_axis=0, tiled=True)]
    unnamed x127 -> x129, local copies, waits for them, and re-layouts: 17.8 us -> 17.2 us
  transfers between devices with their start and end apart: 21 -> 21, of which waited for: 9 -> 8; matrix products, arithmetic and copies ran while one was open for 2% -> 3% of each run, Pallas kernels for 27% -> 28%
where the time goes in v3:
time: 273 us; the launch traced here: 272 us
  Pallas kernels  132 us (48%)
  starting transfers between devices  88 us (32%)
  waiting for transfers between devices  24.9 us (9%)
  local copies, waits for them, and re-layouts  22 us (8%)
  other arithmetic  3.69 us (1%)
    pallas_call x5, Pallas kernels, whole(): pl.pallas_call(kernel, out_shape=outs, in_specs=[pl.BlockSpec(memory_spac...  83.3 us
    all_to_all x7, starting transfers between devices, exchange(): return lax.all_to_all(values, AXES, split_axis=0, concat_axis=0, tiled=True)  63.6 us
    pallas_call x18, Pallas kernels, run(): pl.pallas_call(kernel, out_shape=outs, in_specs=specs + [pl.BlockSpec()]...  48.5 us
    all_to_all x7, waiting for transfers between devices, exchange(): return lax.all_to_all(values, AXES, split_axis=0, concat_axis=0, tiled=True)  18.3 us
    unnamed x129, local copies, waits for them, and re-layouts  17.2 us
    ppermute x4, starting transfers between devices, backward(): lax.ppermute(values, AXES, [((i + 1) % DEVICES, i) for i in range(DEVICES)])  10.6 us
    ppermute x4, starting transfers between devices, shift(): lax.ppermute(values, axis, [(i, (i + step) % count) for i in range(count)])  7.33 us
    ppermute x6, starting transfers between devices, forward(): lax.ppermute(values, AXES, [(i, (i + 1) % DEVICES) for i in range(DEVICES)])  6.43 us
  transfers between devices with their start and end apart: 21, of which 8 were waited for; matrix products, arithmetic and copies ran while one was open for 3% of the time, Pallas kernels for 28%

profile of v3, /device:TPU:1, one launch (start us, length us, event | category | flops | bytes accessed | tf_op | source)
XLA Modules:
  0.0 272.1 jit_solution(11403195366078593079)
XLA Ops:
  0.7 2.8 %shard_map.148 = (f32[2048,128]{1,0:T(8,128)}, f32[8,128]{1,0:T(8,128)}, f32[128,128]{1,0:T(8,128)}) custom-call(s32[1,128]{1,0:T(1,128)} %bitcast.69, f32[3,128,128]{2,1,0:T(8,128)} %bitcast.64, f32[3,128,128]{2,1,0:T(8,128)} %bitcast.65, s32[2,128]{1,0:T(2,128)} %bitcast.68), custom_call_target="tpu_custom_call" | custom-call | tf_op jit(solution)/shard_map/pallas_call | solution.py:551
  3.4 11.5 %all-to-all-start = ((f32[128,16,128]{2,1,0:T(8,128)}), f32[128,16,128]{2,1,0:T(8,128)S(1)}, u32[]{:S(2)}, u32[]{:S(2)}) async-start(f32[128,16,128]{2,1,0:T(8,128)} %bitcast.62), calls=%async_computation | async-start | bytes 2097152 | tf_op jit(solution)/shard_map/all_to_all | solution.py:566
  15.0 1.7 copy-done.3
  16.7 1.7 shard_map.149
  18.4 1.6 collective-permute-start
  20.0 4.0 %collective-permute-start.1 = (f32[40,128]{1,0:T(8,128)S(1)}, f32[40,128]{1,0:T(8,128)S(1)}, u32[]{:S(2)}, u32[]{:S(2)}) collective-permute-start(f32[40,128]{1,0:T(8,128)S(1)} %get-tuple-element.59), channel_id=1, source_target_pairs={{0,120},{8,0},{16,8},{24,16},{32,24},{40,32},{48,40},{56,48},{64,5... | collective-permute-start | bytes 61448 | tf_op jit(solution)/shard_map/ppermute | solution.py:579
  24.0 1.8 collective-permute-start.2
  29.3 4.9 %all-to-all-done = f32[128,16,128]{2,1,0:T(8,128)S(1)} async-done(((f32[128,16,128]{2,1,0:T(8,128)}), f32[128,16,128]{2,1,0:T(8,128)S(1)}, u32[]{:S(2)}, u32[]{:S(2)}) %all-to-all-start) | async-done | bytes 1048608 | tf_op jit(solution)/shard_map/all_to_all | solution.py:566
  35.1 28.8 %shard_map.151 = (bf16[256,256,256]{2,1,0:T(8,128)(2,1)}, f32[256,128]{1,0:T(8,128)}) custom-call(s32[512]{0:T(512)} %reshape.51.support, f32[2048,128]{1,0:T(8,128)} %bitcast.57, bf16[16,128,64]{2,1,0:T(8,128)(2,1)} %copy-done.18, f32[64,128]{1,0:T(8,128)} %pad_bitcast_fusion.3.field.values.extra.last), custom_call_target="tpu_custom_call" | custom-call | flops 2000000000 | bytes 40000000 | tf_op jit(solution)/shard_map/pallas_call | solution.py:590
  64.0 4.6 %all-to-all-start.1 = ((f32[128,2,128]{2,1,0:T(2,128)}), f32[128,2,128]{2,1,0:T(2,128)S(1)}, u32[]{:S(2)}, u32[]{:S(2)}) async-start(f32[128,2,128]{2,1,0:T(2,128)} %bitcast.66), calls=%async_computation.1 | async-start | bytes 262144 | tf_op jit(solution)/shard_map/all_to_all | solution.py:566
  68.6 1.7 collective-permute-start.4
  71.2 2.7 shard_map.155
  73.9 5.3 %collective-permute-start.5 = (f32[64,128]{1,0:T(8,128)}, f32[64,128]{1,0:T(8,128)}, u32[]{:S(2)}, u32[]{:S(2)}) collective-permute-start(f32[64,128]{1,0:T(8,128)} %shard_map.155), channel_id=1, source_target_pairs={{1,0},{2,1},{3,2},{4,3},{5,4},{6,5},{7,6},{8,7},{9,8},{10,9},{11,1... | collective-permute-start | bytes 98312 | tf_op jit(solution)/shard_map/ppermute | solution.py:574
  79.9 1.7 copy-done.4
  81.6 1.5 shard_map.152
  83.1 1.5 shard_map.153
  84.6 5.8 %all-to-all-start.2 = ((f32[128,2,128]{2,1,0:T(2,128)}), f32[128,2,128]{2,1,0:T(2,128)}, u32[]{:S(2)}, u32[]{:S(2)}) async-start(f32[128,2,128]{2,1,0:T(2,128)} %bitcast.12), calls=%async_computation.2 | async-start | bytes 262144 | tf_op jit(solution)/shard_map/all_to_all | solution.py:566
  90.4 1.7 copy-done.5
  92.2 4.8 %shard_map.154 = f32[5,3,128,128]{3,2,1,0:T(8,128)S(1)} custom-call(f32[5,8,128,128]{3,2,1,0:T(8,128)S(1)} %copy-done.5, f32[40,128]{1,0:T(8,128)S(1)} %collective-permute-done.low_x, f32[40,128]{1,0:T(8,128)S(1)} %collective-permute-done.1.high_x, f32[40,128]{1,0:T(8,128)S(1)} %collective-permute-done.2.low_y, f32[40,128]{1,0:T(8,128)S(1)} %collective-permute-done.3.high_y), custom_call_target="tpu_custom_call" | custom-call | flops 120000000 | bytes 2100000 | tf_op jit(solution)/shard_map/pallas_call | solution.py:551
  97.6 2.8 %shard_map.156 = f32[64,128]{1,0:T(8,128)S(1)} custom-call(s32[32]{0:T(128)S(1)} %copy-done.37, f32[64,128]{1,0:T(8,128)S(1)} %copy-done.12, f32[64,128]{1,0:T(8,128)S(1)} %copy-done.42, f32[64,128]{1,0:T(8,128)} %collective-permute-done.5.behind, f32[64,128]{1,0:T(8,128)S(1)} %pad_bitcast_fusion.4.diagonal, f32[8,4,128,128]{3,2,1,0:T(8,128)S(1)} %copy-done), custom_call_target="tpu_custom_call" | custom-call | tf_op jit(solution)/shard_map/pallas_call | solution.py:551
  101.1 18.4 %shard_map.157 = (f32[64,128]{1,0:T(8,128)}, f32[64,128]{1,0:T(8,128)}) custom-call(s32[512]{0:T(512)} %reshape.51.support, s32[32]{0:T(128)} %copy-done.36, f32[256,128]{1,0:T(8,128)} %bitcast.13.amounts, f32[2048,128]{1,0:T(8,128)} %bitcast.58, bf16[256,256,256]{2,1,0:T(8,128)(2,1)} %get-tuple-element.76.phi_hbm, f32[64,128]{1,0:T(8,128)} %fusion.2.base, ...), custom_call_target="tpu_custom_call" | custom-call | flops 2000000000 | bytes 40000000 | tf_op jit(solution)/shard_map/pallas_call | solution.py:590
  119.5 1.8 collective-permute-start.6
  122.6 2.2 collective-permute-done.7.behind
  126.9 2.6 shard_map.158.image
  130.2 8.7 %shard_map.159.more_0_ = f32[128,16,128]{2,1,0:T(8,128)} custom-call(s32[512]{0:T(512)} %reshape.51.support, f32[2048,128]{1,0:T(8,128)} %bitcast.59, f32[64,128]{1,0:T(8,128)} %pad_bitcast_fusion.3.field.values.extra.last, f32[64,128]{1,0:T(8,128)} %get-tuple-element.84.values.start, f32[64,128]{1,0:T(8,128)} %copy-done.16, ...), custom_call_target="tpu_custom_call" | custom-call | flops 2000000000 | bytes 40000000 | tf_op jit(solution)/shard_map/pallas_call | solution.py:590
  139.7 2.8 %shard_map.160 = f32[128,128]{1,0:T(8,128)S(1)} custom-call(s32[32]{0:T(128)S(1)} %copy-done.38, f32[64,128]{1,0:T(8,128)S(1)} %copy-done.15, f32[64,128]{1,0:T(8,128)S(1)} %copy-done.17, f32[64,128]{1,0:T(8,128)S(1)} %collective-permute-done.8.before, f32[64,128]{1,0:T(8,128)S(1)} %pad_bitcast_fusion.4.diagonal, f32[8,4,128,128]{3,2,1,0:T(8,128)S(1)} %copy-done.1, ...), custom_call_target="tpu_custom_call" | custom-call | tf_op jit(solution)/shard_map/pallas_call | solution.py:551
  143.2 13.6 %all-to-all-start.3 = ((f32[128,1,128]{2,1,0:T(1,128)}), f32[128,1,128]{2,1,0:T(1,128)}, u32[]{:S(2)}, u32[]{:S(2)}) async-start(f32[128,1,128]{2,1,0:T(1,128)} %bitcast.54), calls=%async_computation.3 | async-start | bytes 131072 | tf_op jit(solution)/shard_map/all_to_all | solution.py:566
  156.8 8.7 %shard_map.161.more_1_ = f32[128,16,128]{2,1,0:T(8,128)} custom-call(s32[512]{0:T(512)} %reshape.51.support, f32[2048,128]{1,0:T(8,128)} %bitcast.60, f32[64,128]{1,0:T(8,128)} %pad_bitcast_fusion.3.field.values.extra.last, f32[64,128]{1,0:T(8,128)} %get-tuple-element.84.values.start, f32[64,128]{1,0:T(8,128)} %copy-done.16, ...), custom_call_target="tpu_custom_call" | custom-call | flops 2000000000 | bytes 40000000 | tf_op jit(solution)/shard_map/pallas_call | solution.py:590
  166.6 3.8 %shard_map.162 = (f32[64,128]{1,0:T(8,128)}, f32[64,128]{1,0:T(8,128)}, f32[64,128]{1,0:T(8,128)}, f32[16,128]{1,0:T(8,128)}, f32[256,128]{1,0:T(8,128)}) custom-call(f32[128,128]{1,0:T(8,128)} %bitcast.22.received, f32[16,128]{1,0:T(8,128)} %broadcast_in_dim.16.memory, f32[64,128]{1,0:T(8,128)} %pad_bitcast_fusion.3.field.values.extra.last, ...), custom_call_target="tpu_custom_call" | custom-call | tf_op jit(solution)/shard_map/pallas_call | solution.py:551
  170.4 9.8 %all-to-all-start.4 = ((f32[128,2,128]{2,1,0:T(2,128)}), f32[128,2,128]{2,1,0:T(2,128)}, u32[]{:S(2)}, u32[]{:S(2)}) async-start(f32[128,2,128]{2,1,0:T(2,128)} %bitcast.67), calls=%async_computation.4 | async-start | bytes 262144 | tf_op jit(solution)/shard_map/all_to_all | solution.py:566
  180.2 1.7 collective-permute-start.9
  182.7 2.7 shard_map.164
  186.0 5.3 %collective-permute-start.10 = (f32[64,128]{1,0:T(8,128)}, f32[64,128]{1,0:T(8,128)}, u32[]{:S(2)}, u32[]{:S(2)}) collective-permute-start(f32[64,128]{1,0:T(8,128)} %shard_map.164), channel_id=1, source_target_pairs={{1,0},{2,1},{3,2},{4,3},{5,4},{6,5},{7,6},{8,7},{9,8},{10,9},{11,1... | collective-permute-start | bytes 98312 | tf_op jit(solution)/shard_map/ppermute | solution.py:574
  192.2 1.7 shard_map.163
  195.3 4.8 %all-to-all-start.5 = ((f32[128,2,128]{2,1,0:T(2,128)}), f32[128,2,128]{2,1,0:T(2,128)S(1)}, u32[]{:S(2)}, u32[]{:S(2)}) async-start(f32[128,2,128]{2,1,0:T(2,128)} %bitcast.55), calls=%async_computation.5 | async-start | bytes 262144 | tf_op jit(solution)/shard_map/all_to_all | solution.py:566
  200.9 2.8 %shard_map.165 = f32[64,128]{1,0:T(8,128)S(1)} custom-call(s32[32]{0:T(128)S(1)} %copy-done.38, f32[64,128]{1,0:T(8,128)S(1)} %copy-done.21, f32[64,128]{1,0:T(8,128)S(1)} %copy-done.44, f32[64,128]{1,0:T(8,128)} %collective-permute-done.10.behind, f32[64,128]{1,0:T(8,128)S(1)} %pad_bitcast_fusion.4.diagonal, f32[8,4,128,128]{3,2,1,0:T(8,128)S(1)} %copy-done.1), custom_call_target="tpu_custom_call" | custom-call | tf_op jit(solution)/shard_map/pallas_call | solution.py:551
  203.8 1.3 fusion.1.base
  205.1 5.1 %all-to-all-done.5 = f32[128,2,128]{2,1,0:T(2,128)S(1)} async-done(((f32[128,2,128]{2,1,0:T(2,128)}), f32[128,2,128]{2,1,0:T(2,128)S(1)}, u32[]{:S(2)}, u32[]{:S(2)}) %all-to-all-start.5) | async-done | bytes 131104 | tf_op jit(solution)/shard_map/all_to_all | solution.py:566
  210.9 18.7 %shard_map.166 = (f32[64,128]{1,0:T(8,128)}, f32[64,128]{1,0:T(8,128)}) custom-call(s32[512]{0:T(512)} %reshape.51.support, s32[32]{0:T(128)} %copy-done.36, f32[256,128]{1,0:T(8,128)} %bitcast.63, f32[2048,128]{1,0:T(8,128)} %bitcast.61, bf16[256,256,256]{2,1,0:T(8,128)(2,1)} %get-tuple-element.76.phi_hbm, f32[64,128]{1,0:T(8,128)} %fusion.1.base, ...), custom_call_target="tpu_custom_call" | custom-call | flops 2000000000 | bytes 40000000 | tf_op jit(solution)/shard_map/pallas_call | solution.py:590
  230.3 1.3 collective-permute-done.11.before
  231.7 2.2 collective-permute-done.12.behind
  234.7 2.6 shard_map.167.image
  237.5 6.2 %shard_map.168 = f32[5,4,128,128]{3,2,1,0:T(8,128)S(1)} custom-call(f32[5,8,128,128]{3,2,1,0:T(8,128)S(1)} %copy-done.6, f32[40,128]{1,0:T(8,128)S(1)} %copy-done.28, f32[40,128]{1,0:T(8,128)S(1)} %copy-done.30, f32[40,128]{1,0:T(8,128)S(1)} %copy-done.32, f32[40,128]{1,0:T(8,128)S(1)} %copy-done.34), custom_call_target="tpu_custom_call" | custom-call | flops 160000000 | bytes 2800000 | tf_op jit(solution)/shard_map/pallas_call | solution.py:551
  243.8 3.5 %shard_map.169 = f32[128,128]{1,0:T(8,128)} custom-call(s32[32]{0:T(128)S(1)} %copy-done.39, f32[64,128]{1,0:T(8,128)S(1)} %copy-done.23, f32[64,128]{1,0:T(8,128)S(1)} %shard_map.167.image, f32[64,128]{1,0:T(8,128)S(1)} %collective-permute-done.13.before, f32[64,128]{1,0:T(8,128)S(1)} %pad_bitcast_fusion.4.diagonal, f32[8,4,128,128]{3,2,1,0:T(8,128)S(1)} %copy-done.2, ...), custom_call_target="tpu_custom_call" | custom-call | tf_op jit(solution)/shard_map/pallas_call | solution.py:551
  247.2 13.6 %all-to-all-start.6 = ((f32[128,1,128]{2,1,0:T(1,128)}), f32[128,1,128]{2,1,0:T(1,128)S(1)}, u32[]{:S(2)}, u32[]{:S(2)}) async-start(f32[128,1,128]{2,1,0:T(1,128)} %bitcast.29), calls=%async_computation.6 | async-start | bytes 131072 | tf_op jit(solution)/shard_map/all_to_all | solution.py:566
  260.9 1.7 pad_maximum_fusion
  262.6 7.8 %all-to-all-done.6 = f32[128,1,128]{2,1,0:T(1,128)S(1)} async-done(((f32[128,1,128]{2,1,0:T(1,128)}), f32[128,1,128]{2,1,0:T(1,128)S(1)}, u32[]{:S(2)}, u32[]{:S(2)}) %all-to-all-start.6) | async-done | bytes 65568 | tf_op jit(solution)/shard_map/all_to_all | solution.py:566
  270.4 1.7 shard_map.170
  (163 shorter events, 20.6 us)
Async XLA Ops:
  0.6 25.1 %copy-start.58 = (f32[8,3,128]{2,0,1:T(8,128)S(1)}, f32[8,3,128]{2,0,1:T(8,128)}, u32[]{:S(2)}) copy-start(f32[8,3,128]{2,0,1:T(8,128)} %param.23) | copy-start | bytes 36868
  0.6 25.1 %copy-start.50 = (f32[8,3,128]{2,0,1:T(8,128)S(1)}, f32[8,3,128]{2,0,1:T(8,128)}, u32[]{:S(2)}) copy-start(f32[8,3,128]{2,0,1:T(8,128)} %param.18) | copy-start | bytes 36868
  3.4 23.4 %copy-start.57 = (f32[8,8,3,128]{3,1,2,0:T(8,128)S(1)}, f32[8,8,3,128]{3,1,2,0:T(8,128)}, u32[]{:S(2)}) copy-start(f32[8,8,3,128]{3,1,2,0:T(8,128)} %param.25) | copy-start | bytes 294916
  3.4 23.4 %copy-start.54 = (f32[8,8,3,128]{3,1,2,0:T(8,128)S(1)}, f32[8,8,3,128]{3,1,2,0:T(8,128)}, u32[]{:S(2)}) copy-start(f32[8,8,3,128]{3,1,2,0:T(8,128)} %param.24) | copy-start | bytes 294916
  3.4 30.7 %all-to-all-start = ((f32[128,16,128]{2,1,0:T(8,128)}), f32[128,16,128]{2,1,0:T(8,128)S(1)}, u32[]{:S(2)}, u32[]{:S(2)}) async-start(f32[128,16,128]{2,1,0:T(8,128)} %bitcast.62), calls=%async_computation | async-start | bytes 2097152 | tf_op jit(solution)/shard_map/all_to_all | solution.py:566
  18.4 45.5 %collective-permute-start = (f32[40,128]{1,0:T(8,128)S(1)}, f32[40,128]{1,0:T(8,128)S(1)}, u32[]{:S(2)}, u32[]{:S(2)}) collective-permute-start(f32[40,128]{1,0:T(8,128)S(1)} %get-tuple-element.58), channel_id=1, source_target_pairs={{0,8},{8,16},{16,24},{24,32},{32,40},{40,48},{48,56},{56,64},{64,7... | collective-permute-start | bytes 61448 | tf_op jit(solution)/shard_map/ppermute | solution.py:579
  20.0 44.0 %collective-permute-start.1 = (f32[40,128]{1,0:T(8,128)S(1)}, f32[40,128]{1,0:T(8,128)S(1)}, u32[]{:S(2)}, u32[]{:S(2)}) collective-permute-start(f32[40,128]{1,0:T(8,128)S(1)} %get-tuple-element.59), channel_id=1, source_target_pairs={{0,120},{8,0},{16,8},{24,16},{32,24},{40,32},{48,40},{56,48},{64,5... | collective-permute-start | bytes 61448 | tf_op jit(solution)/shard_map/ppermute | solution.py:579
  24.0 40.0 %collective-permute-start.2 = (f32[40,128]{1,0:T(8,128)S(1)}, f32[40,128]{1,0:T(8,128)S(1)}, u32[]{:S(2)}, u32[]{:S(2)}) collective-permute-start(f32[40,128]{1,0:T(8,128)S(1)} %get-tuple-element.60), channel_id=1, source_target_pairs={{0,1},{1,2},{2,3},{3,4},{4,5},{5,6},{6,7},{7,0},{8,9},{9,10},{10,1... | collective-permute-start | bytes 61448 | tf_op jit(solution)/shard_map/ppermute | solution.py:579
  25.8 38.2 %collective-permute-start.3 = (f32[40,128]{1,0:T(8,128)S(1)}, f32[40,128]{1,0:T(8,128)S(1)}, u32[]{:S(2)}, u32[]{:S(2)}) collective-permute-start(f32[40,128]{1,0:T(8,128)S(1)} %get-tuple-element.61), channel_id=1, source_target_pairs={{0,7},{1,0},{2,1},{3,2},{4,3},{5,4},{6,5},{7,6},{8,15},{9,8},{10,9... | collective-permute-start | bytes 61448 | tf_op jit(solution)/shard_map/ppermute | solution.py:579
  29.2 53.9 %copy-start.8 = (f32[5,128,128]{2,1,0:T(8,128)}, f32[5,128,128]{2,1,0:T(8,128)S(1)}, u32[]{:S(2)}) copy-start(f32[5,128,128]{2,1,0:T(8,128)S(1)} %slice_bitcast_fusion.bottom) | copy-start | bytes 983044
  35.1 33.5 %copy-start.12 = (f32[64,128]{1,0:T(8,128)S(1)}, f32[64,128]{1,0:T(8,128)}, u32[]{:S(2)}) copy-start(f32[64,128]{1,0:T(8,128)} %pad_bitcast_fusion.3.field.values.extra.last) | copy-start | bytes 98308
  35.1 35.9 %copy-start.61 = (s32[8,4]{0,1:T(4,128)S(1)}, s32[8,4]{0,1:T(4,128)}, u32[]{:S(2)}) copy-start(s32[8,4]{0,1:T(4,128)} %param.20) | copy-start | bytes 388
  35.1 36.1 %copy-start = (f32[8,4,128,128]{3,2,1,0:T(8,128)S(1)}, f32[8,4,128,128]{3,2,1,0:T(8,128)}, u32[]{:S(2)}) copy-start(f32[8,4,128,128]{3,2,1,0:T(8,128)} %couplings.19) | copy-start | bytes 6291460
  63.9 15.3 %copy-start.60 = (f32[8,128]{1,0:T(8,128)S(1)}, f32[8,128]{1,0:T(8,128)}, u32[]{:S(2)}) copy-start(f32[8,128]{1,0:T(8,128)} %param.21) | copy-start | bytes 12292
  63.9 15.3 %copy-start.59 = (f32[8,3,128]{2,0,1:T(8,128)S(1)}, f32[8,3,128]{2,0,1:T(8,128)}, u32[]{:S(2)}) copy-start(f32[8,3,128]{2,0,1:T(8,128)} %param.22) | copy-start | bytes 36868
  63.9 26.4 %copy-start.27 = (f32[40,128]{1,0:T(8,128)}, f32[40,128]{1,0:T(8,128)S(1)}, u32[]{:S(2)}) copy-start(f32[40,128]{1,0:T(8,128)S(1)} %collective-permute-done.low_x) | copy-start | bytes 61444
  64.0 26.4 %copy-start.29 = (f32[40,128]{1,0:T(8,128)}, f32[40,128]{1,0:T(8,128)S(1)}, u32[]{:S(2)}) copy-start(f32[40,128]{1,0:T(8,128)S(1)} %collective-permute-done.1.high_x) | copy-start | bytes 61444
  64.0 26.4 %copy-start.31 = (f32[40,128]{1,0:T(8,128)}, f32[40,128]{1,0:T(8,128)S(1)}, u32[]{:S(2)}) copy-start(f32[40,128]{1,0:T(8,128)S(1)} %collective-permute-done.2.low_y) | copy-start | bytes 61444
  64.0 26.4 %copy-start.33 = (f32[40,128]{1,0:T(8,128)}, f32[40,128]{1,0:T(8,128)S(1)}, u32[]{:S(2)}) copy-start(f32[40,128]{1,0:T(8,128)S(1)} %collective-permute-done.3.high_y) | copy-start | bytes 61444
  64.0 19.1 %all-to-all-start.1 = ((f32[128,2,128]{2,1,0:T(2,128)}), f32[128,2,128]{2,1,0:T(2,128)S(1)}, u32[]{:S(2)}, u32[]{:S(2)}) async-start(f32[128,2,128]{2,1,0:T(2,128)} %bitcast.66), calls=%async_computation.1 | async-start | bytes 262144 | tf_op jit(solution)/shard_map/all_to_all | solution.py:566
  68.6 5.3 %collective-permute-start.4 = (f32[64,128]{1,0:T(8,128)S(1)}, f32[64,128]{1,0:T(8,128)S(1)}, u32[]{:S(2)}, u32[]{:S(2)}) collective-permute-start(f32[64,128]{1,0:T(8,128)S(1)} %copy-done.12), channel_id=1, source_target_pairs={{0,1},{1,2},{2,3},{3,4},{4,5},{5,6},{6,7},{7,8},{8,9},{9,10},{10,1... | collective-permute-start | bytes 98312 | tf_op jit(solution)/shard_map/ppermute | solution.py:570
  73.9 23.1 %collective-permute-start.5 = (f32[64,128]{1,0:T(8,128)}, f32[64,128]{1,0:T(8,128)}, u32[]{:S(2)}, u32[]{:S(2)}) collective-permute-start(f32[64,128]{1,0:T(8,128)} %shard_map.155), channel_id=1, source_target_pairs={{1,0},{2,1},{3,2},{4,3},{5,4},{6,5},{7,6},{8,7},{9,8},{10,9},{11,1... | collective-permute-start | bytes 98312 | tf_op jit(solution)/shard_map/ppermute | solution.py:574
  84.6 16.5 %all-to-all-start.2 = ((f32[128,2,128]{2,1,0:T(2,128)}), f32[128,2,128]{2,1,0:T(2,128)}, u32[]{:S(2)}, u32[]{:S(2)}) async-start(f32[128,2,128]{2,1,0:T(2,128)} %bitcast.12), calls=%async_computation.2 | async-start | bytes 262144 | tf_op jit(solution)/shard_map/all_to_all | solution.py:566
  101.1 20.1 %copy-start.55 = (f32[8,8,3,128]{3,1,2,0:T(8,128)S(1)}, f32[8,8,3,128]{3,1,2,0:T(8,128)}, u32[]{:S(2)}) copy-start(f32[8,8,3,128]{3,1,2,0:T(8,128)} %param.24) | copy-start | bytes 294916
  101.1 24.3 %copy-start.1 = (f32[8,4,128,128]{3,2,1,0:T(8,128)S(1)}, f32[8,4,128,128]{3,2,1,0:T(8,128)}, u32[]{:S(2)}) copy-start(f32[8,4,128,128]{3,2,1,0:T(8,128)} %couplings.19) | copy-start | bytes 6291460
  101.1 24.3 %copy-start.38 = (s32[32]{0:T(128)S(1)}, s32[32]{0:T(128)}, u32[]{:S(2)}) copy-start(s32[32]{0:T(128)} %copy-done.36) | copy-start | bytes 388
  119.5 3.1 %collective-permute-start.6 = (f32[64,128]{1,0:T(8,128)}, f32[64,128]{1,0:T(8,128)S(1)}, u32[]{:S(2)}, u32[]{:S(2)}) collective-permute-start(f32[64,128]{1,0:T(8,128)} %get-tuple-element.84.values.start), channel_id=1, source_target_pairs={{0,1},{1,2},{2,3},{3,4},{4,5},{5,6},{6,7},{7,8},{8,9},{9,10},{10,1... | collective-permute-start | bytes 98312 | tf_op jit(solution)/shard_map/ppermute | solution.py:570
  121.3 3.6 %collective-permute-start.7 = (f32[64,128]{1,0:T(8,128)}, f32[64,128]{1,0:T(8,128)S(1)}, u32[]{:S(2)}, u32[]{:S(2)}) collective-permute-start(f32[64,128]{1,0:T(8,128)} %get-tuple-element.82), channel_id=1, source_target_pairs={{1,0},{2,1},{3,2},{4,3},{5,4},{6,5},{7,6},{8,7},{9,8},{10,9},{11,1... | collective-permute-start | bytes 98312 | tf_op jit(solution)/shard_map/ppermute | solution.py:574
  129.6 9.3 %collective-permute-start.8 = (f32[64,128]{1,0:T(8,128)S(1)}, f32[64,128]{1,0:T(8,128)S(1)}, u32[]{:S(2)}, u32[]{:S(2)}) collective-permute-start(f32[64,128]{1,0:T(8,128)S(1)} %shard_map.158.image), channel_id=1, source_target_pairs={{0,1},{1,2},{2,3},{3,4},{4,5},{5,6},{6,7},{7,8},{8,9},{9,10},{10,1... | collective-permute-start | bytes 98312 | tf_op jit(solution)/shard_map/ppermute | solution.py:570
  143.2 22.8 %all-to-all-start.3 = ((f32[128,1,128]{2,1,0:T(1,128)}), f32[128,1,128]{2,1,0:T(1,128)}, u32[]{:S(2)}, u32[]{:S(2)}) async-start(f32[128,1,128]{2,1,0:T(1,128)} %bitcast.54), calls=%async_computation.3 | async-start | bytes 131072 | tf_op jit(solution)/shard_map/all_to_all | solution.py:566
  165.5 25.7 %copy-start.26 = (f32[128,128]{1,0:T(8,128)S(1)}, f32[128,128]{1,0:T(8,128)}, u32[]{:S(2)}) copy-start(f32[128,128]{1,0:T(8,128)} %get-tuple-element.65.slot_col) | copy-start | bytes 196612
  165.5 25.7 %copy-start.49 = (f32[8,128]{1,0:T(8,128)S(1)}, f32[8,128]{1,0:T(8,128)}, u32[]{:S(2)}) copy-start(f32[8,128]{1,0:T(8,128)} %get-tuple-element.64.slot_row) | copy-start | bytes 12292
  170.4 20.8 %all-to-all-start.4 = ((f32[128,2,128]{2,1,0:T(2,128)}), f32[128,2,128]{2,1,0:T(2,128)}, u32[]{:S(2)}, u32[]{:S(2)}) async-start(f32[128,2,128]{2,1,0:T(2,128)} %bitcast.67), calls=%async_computation.4 | async-start | bytes 262144 | tf_op jit(solution)/shard_map/all_to_all | solution.py:566
  180.2 5.2 %collective-permute-start.9 = (f32[64,128]{1,0:T(8,128)}, f32[64,128]{1,0:T(8,128)S(1)}, u32[]{:S(2)}, u32[]{:S(2)}) collective-permute-start(f32[64,128]{1,0:T(8,128)} %get-tuple-element.95.values.field), channel_id=1, source_target_pairs={{0,1},{1,2},{2,3},{3,4},{4,5},{5,6},{6,7},{7,8},{8,9},{9,10},{10,1... | collective-permute-start | bytes 98312 | tf_op jit(solution)/shard_map/ppermute | solution.py:570
  186.0 14.2 %collective-permute-start.10 = (f32[64,128]{1,0:T(8,128)}, f32[64,128]{1,0:T(8,128)}, u32[]{:S(2)}, u32[]{:S(2)}) collective-permute-start(f32[64,128]{1,0:T(8,128)} %shard_map.164), channel_id=1, source_target_pairs={{1,0},{2,1},{3,2},{4,3},{5,4},{6,5},{7,6},{8,7},{9,8},{10,9},{11,1... | collective-permute-start | bytes 98312 | tf_op jit(solution)/shard_map/ppermute | solution.py:574
  195.3 14.9 %all-to-all-start.5 = ((f32[128,2,128]{2,1,0:T(2,128)}), f32[128,2,128]{2,1,0:T(2,128)S(1)}, u32[]{:S(2)}, u32[]{:S(2)}) async-start(f32[128,2,128]{2,1,0:T(2,128)} %bitcast.55), calls=%async_computation.5 | async-start | bytes 262144 | tf_op jit(solution)/shard_map/all_to_all | solution.py:566
  210.9 23.0 %copy-start.2 = (f32[8,4,128,128]{3,2,1,0:T(8,128)S(1)}, f32[8,4,128,128]{3,2,1,0:T(8,128)}, u32[]{:S(2)}) copy-start(f32[8,4,128,128]{3,2,1,0:T(8,128)} %couplings.19) | copy-start | bytes 6291460
  210.9 23.0 %copy-start.39 = (s32[32]{0:T(128)S(1)}, s32[32]{0:T(128)}, u32[]{:S(2)}) copy-start(s32[32]{0:T(128)} %copy-done.36) | copy-start | bytes 388
  210.9 26.6 %copy-start.6 = (f32[5,8,128,128]{3,2,1,0:T(8,128)S(1)}, f32[5,8,128,128]{3,2,1,0:T(8,128)}, u32[]{:S(2)}) copy-start(f32[5,8,128,128]{3,2,1,0:T(8,128)} %state.7) | copy-start | bytes 7864324
  210.9 26.6 %copy-start.28 = (f32[40,128]{1,0:T(8,128)S(1)}, f32[40,128]{1,0:T(8,128)}, u32[]{:S(2)}) copy-start(f32[40,128]{1,0:T(8,128)} %copy-done.27) | copy-start | bytes 61444
  210.9 26.6 %copy-start.30 = (f32[40,128]{1,0:T(8,128)S(1)}, f32[40,128]{1,0:T(8,128)}, u32[]{:S(2)}) copy-start(f32[40,128]{1,0:T(8,128)} %copy-done.29) | copy-start | bytes 61444
  210.9 26.6 %copy-start.32 = (f32[40,128]{1,0:T(8,128)S(1)}, f32[40,128]{1,0:T(8,128)}, u32[]{:S(2)}) copy-start(f32[40,128]{1,0:T(8,128)} %copy-done.31) | copy-start | bytes 61444
  210.9 26.6 %copy-start.34 = (f32[40,128]{1,0:T(8,128)S(1)}, f32[40,128]{1,0:T(8,128)}, u32[]{:S(2)}) copy-start(f32[40,128]{1,0:T(8,128)} %copy-done.33) | copy-start | bytes 61444
  229.6 2.1 collective-permute-start.11
  230.3 3.6 %collective-permute-start.12 = (f32[64,128]{1,0:T(8,128)}, f32[64,128]{1,0:T(8,128)S(1)}, u32[]{:S(2)}, u32[]{:S(2)}) collective-permute-start(f32[64,128]{1,0:T(8,128)} %get-tuple-element.99), channel_id=1, source_target_pairs={{1,0},{2,1},{3,2},{4,3},{5,4},{6,5},{7,6},{8,7},{9,8},{10,9},{11,1... | collective-permute-start | bytes 98312 | tf_op jit(solution)/shard_map/ppermute | solution.py:574
  237.3 23.6 %copy-start.20 = (f32[5,128,128]{2,1,0:T(8,128)S(1)}, f32[5,128,128]{2,1,0:T(8,128)}, u32[]{:S(2)}) copy-start(f32[5,128,128]{2,1,0:T(8,128)} %copy-done.19) | copy-start | bytes 983044
  237.3 6.4 %collective-permute-start.13 = (f32[64,128]{1,0:T(8,128)S(1)}, f32[64,128]{1,0:T(8,128)S(1)}, u32[]{:S(2)}, u32[]{:S(2)}) collective-permute-start(f32[64,128]{1,0:T(8,128)S(1)} %shard_map.167.image), channel_id=1, source_target_pairs={{0,1},{1,2},{2,3},{3,4},{4,5},{5,6},{6,7},{7,8},{8,9},{9,10},{10,1... | collective-permute-start | bytes 98312 | tf_op jit(solution)/shard_map/ppermute | solution.py:570
  247.2 23.1 %all-to-all-start.6 = ((f32[128,1,128]{2,1,0:T(1,128)}), f32[128,1,128]{2,1,0:T(1,128)S(1)}, u32[]{:S(2)}, u32[]{:S(2)}) async-start(f32[128,1,128]{2,1,0:T(1,128)} %bitcast.29), calls=%async_computation.6 | async-start | bytes 131072 | tf_op jit(solution)/shard_map/all_to_all | solution.py:566
  (35 other events, 161.4 us)
